TPU v7x, 32 devices: a whole 2x2x4 slice. The times are simulated.
32 devices in a mesh: seq: 16 (over z, y, core), rows: 2 (over x).
Axes of the slice: x: 2, y: 2, z: 4, core: 2. Of those that a mesh axis runs over, the one named last changes fastest.
Arguments:
- tokens: bfloat16 [32, 16, 64, 1152], P('seq', 'rows'), may hold values from -6 to 6
- image_ids: int32 [32, 64], P('seq'), may hold values from 0 to 3, as said below
- timestep: int32 [32, 4], P('seq'), may hold values from 0 to 999
- norm1_gain: float32 [1152], replicated, may hold values from 0.1 to 1.9
- norm1_shift: float32 [1152], replicated, may hold values from -3 to 3
- time_in_weight: bfloat16 [256, 1152], P('seq'), may hold values from -0.375 to 0.375
- time_in_bias: float32 [1152], replicated, may hold values from -3 to 3
- time_out_weight: bfloat16 [1152, 1152], P('seq'), may hold values from -0.1875 to 0.1875
- time_out_bias: float32 [1152], replicated, may hold values from -3 to 3
- mix_weight: bfloat16 [1152, 3456], P('seq'), may hold values from -0.1875 to 0.1875
- time_mix_weight: bfloat16 [1152, 3456], P('seq'), may hold values from -0.1875 to 0.1875
- position_bias: float32 [16, 9, 9], replicated, may hold values from -4 to 4
- proj_weight: bfloat16 [1152, 1152], P('seq'), may hold values from -0.5 to 0.5
- proj_bias: float32 [1152], replicated, may hold values from -2 to 2
- norm2_gain: float32 [1152], replicated, may hold values from 0.1 to 1.9
- norm2_shift: float32 [1152], replicated, may hold values from -3 to 3
- up_weight: bfloat16 [1152, 4608], P('seq'), may hold values from -0.1875 to 0.1875
- up_bias: float32 [4608], replicated, may hold values from -3 to 3
- down_weight: bfloat16 [4608, 1152], P('seq'), may hold values from -0.09375 to 0.09375
- down_bias: float32 [1152], replicated, may hold values from -2 to 2
- cotangent: bfloat16 [32, 16, 64, 1152], P('seq', 'rows'), may hold values from -6 to 6
Outputs:
- output: bfloat16 [32, 16, 64, 1152], P('seq', 'rows')
- tokens_grad: bfloat16 [32, 16, 64, 1152], P('seq', 'rows')
- norm1_gain_grad: float32 [1152], replicated
- norm1_shift_grad: float32 [1152], replicated
- time_in_weight_grad: float32 [256, 1152], P('seq')
- time_in_bias_grad: float32 [1152], replicated
- time_out_weight_grad: float32 [1152, 1152], P('seq')
- time_out_bias_grad: float32 [1152], replicated
- mix_weight_grad: float32 [1152, 3456], P('seq')
- time_mix_weight_grad: float32 [1152, 3456], P('seq')
- position_bias_grad: float32 [16, 9, 9], replicated
- proj_weight_grad: float32 [1152, 1152], P('seq')
- proj_bias_grad: float32 [1152], replicated
- norm2_gain_grad: float32 [1152], replicated
- norm2_shift_grad: float32 [1152], replicated
- up_weight_grad: float32 [1152, 4608], P('seq')
- up_bias_grad: float32 [4608], replicated
- down_weight_grad: float32 [4608, 1152], P('seq')
- down_bias_grad: float32 [1152], replicated
Inputs may be any that keep to these rules, and one draw needn't show every extreme that they name: `image_ids`: canvas columns k * 16 to (k + 1) * 16 - 1 of a sequence row share one id, and the 4 blocks of a row hold each id once.
All inputs are finite; a program needn't handle non-finite values.
Results may differ from a plain program's by a relative error of at most 0.019.
Values may be sent and summed in bfloat16 or wider, within the bound.
No kernel may reach another device: no remote copies, remote signals or barrier semaphores. Data moves between devices by JAX's collectives and lax.ppermute only.
A program may use at most 640 MiB of HBM per device.

v0:
```python
import functools
import math

import jax
import jax.numpy as jnp
from jax import lax
from jax.experimental import pallas as pl
from jax.experimental.pallas import tpu as pltpu
from jax.sharding import PartitionSpec as P

D = 1152
HEADS = 16
HEAD_DIM = 72
FF = 4608
FREQ = 256
GRID = 16
PACK = 4
REACH = 4
LANES = 128


epsilon = 1e-06
floor_score = -1e30
highest = lax.Precision.HIGHEST
score_scale = HEAD_DIM ** (-0.5)


def low_dot(left, right):
    return jnp.dot(left, right, preferred_element_type=jnp.float32)


def norm_forward(values, norm_gain, norm_shift):
    centred = values - jnp.mean(values, axis=-1, keepdims=True)
    inverse = lax.rsqrt(jnp.mean(centred * centred, axis=-1, keepdims=True) + epsilon)
    unit_rows = centred * inverse
    return (unit_rows * norm_gain + norm_shift, unit_rows, inverse)


def norm_backward(grad_out, unit_rows, inverse, norm_gain):
    scaled = grad_out * norm_gain
    grad_in = inverse * (
        scaled
        - jnp.mean(scaled, axis=-1, keepdims=True)
        - unit_rows * jnp.mean(scaled * unit_rows, axis=-1, keepdims=True)
    )
    leading = tuple(range(grad_out.ndim - 1))
    return (grad_in, jnp.sum(grad_out * unit_rows, axis=leading), jnp.sum(grad_out, axis=leading))


def row_plan(local_rows, shards):
    if shards == 2 and local_rows >= REACH:
        return (True, 1, REACH)
    sent = min(local_rows, REACH)
    return (False, -(-REACH // local_rows), sent)


def route(shards, distance):
    return [(i - distance, i) for i in range(shards) if 0 <= i - distance < shards]


def borrow_rows(own, shards):
    rows = own.shape[1]
    one_sided, turns, sent = row_plan(rows, shards)
    place = lax.axis_index("rows")
    if one_sided:
        start = jnp.where(place == 0, rows - sent, 0)
        block = lax.dynamic_slice_in_dim(own, start, sent, axis=1)
        got = lax.ppermute(block, "rows", [(0, 1), (1, 0)])
        first = jnp.where(place == 0, rows, -sent)
        return (got, first + jnp.arange(sent), block)
    pieces, where = [], []
    for turn in range(turns, 0, -1):
        pieces.append(lax.ppermute(own[:, rows - sent :], "rows", route(shards, turn)))
        where.append(jnp.arange(sent) - (turn - 1) * rows - sent)
    for turn in range(1, turns + 1):
        pieces.append(lax.ppermute(own[:, :sent], "rows", route(shards, -turn)))
        where.append(jnp.arange(sent) + turn * rows)
    return (jnp.concatenate(pieces, axis=1), jnp.concatenate(where), own[:, :sent])


def head_window(head):
    first, last = head * HEAD_DIM, (head + 1) * HEAD_DIM
    return (first // LANES * LANES, -(-last // LANES) * LANES)


def head_mask(head, dtype):
    low, high = head_window(head)
    lane = lax.broadcasted_iota(jnp.int32, (1, high - low), 1) + low
    return ((lane >= head * HEAD_DIM) & (lane < (head + 1) * HEAD_DIM)).astype(dtype)


def nt_dot(left, right):
    return lax.dot_general(left, right, (((1,), (1,)), ((), ())), preferred_element_type=jnp.float32)


def tn_dot(left, right):
    return lax.dot_general(left, right, (((0,), (0,)), ((), ())), preferred_element_type=jnp.float32)


def table_kernel(bias_ref, row_ref, out_ref, *, own, rows):
    head = pl.program_id(0)
    reach = 2 * REACH + 1
    lane = lax.broadcasted_iota(jnp.int32, (GRID, own), 1)
    query_row, query_col = lane // GRID, lane % GRID
    col_diff = lax.broadcasted_iota(jnp.int32, (GRID, own), 0) - query_col
    floor = jnp.full((GRID, own), floor_score, jnp.float32)
    by_row = []
    for n in range(reach):
        value = floor
        for o in range(reach):
            value = jnp.where(col_diff == o - REACH, bias_ref[head, n * reach + o], value)
        by_row.append(value)
    for b in range(rows):
        row_diff = row_ref[b] - query_row
        value = floor
        for n in range(reach):
            value = jnp.where(row_diff == n - REACH, by_row[n], value)
        out_ref[0, b * GRID : (b + 1) * GRID, :] = value


def bias_table(position_bias, key_rows, own_rows):
    rows = key_rows.shape[0]
    own, total = own_rows * GRID, rows * GRID
    smem = pl.BlockSpec(memory_space=pltpu.SMEM)
    return pl.pallas_call(
        functools.partial(table_kernel, own=own, rows=rows),
        grid=(HEADS,),
        in_specs=[smem, smem],
        out_specs=pl.BlockSpec((1, total, own), lambda h: (h, 0, 0)),
        out_shape=jax.ShapeDtypeStruct((HEADS, total, own), jnp.float32),
        name="bias_table",
    )(position_bias.reshape(HEADS, -1), key_rows)


def assemble_kernel(at_ref, *refs, count):
    pieces, out_ref, room, into, out_of = refs[:count], refs[-4], refs[-3], refs[-2], refs[-1]
    first = [pltpu.make_async_copy(piece, room.at[i], into.at[i]) for i, piece in enumerate(pieces)]
    second = [pltpu.make_async_copy(room.at[i], out_ref.at[at_ref[i]], out_of.at[i]) for i in range(len(pieces))]
    for copy in first:
        copy.start()
    for one, two in zip(first, second):
        one.wait()
        two.start()
    for copy in second:
        copy.wait()


def assemble(pieces, at, size, kept=None):
    anywhere = pl.BlockSpec(memory_space=pl.ANY)
    shape, dtype, count = pieces[0].shape, pieces[0].dtype, len(pieces)
    return pl.pallas_call(
        functools.partial(assemble_kernel, count=len(pieces)),
        grid_spec=pltpu.PrefetchScalarGridSpec(
            num_scalar_prefetch=1,
            grid=(1,),
            in_specs=[anywhere] * (count if kept is None else count + 1),
            out_specs=anywhere,
            scratch_shapes=[
                pltpu.VMEM((count,) + shape, dtype),
                pltpu.SemaphoreType.DMA((count,)),
                pltpu.SemaphoreType.DMA((count,)),
            ],
        ),
        out_shape=jax.ShapeDtypeStruct((size,) + shape, dtype),
        input_output_aliases={} if kept is None else {count + 1: 0},
        compiler_params=pltpu.CompilerParams(vmem_limit_bytes=48 << 20),
        name="assemble",
    )(at, *pieces, *(() if kept is None else (kept,)))


def bias_sum_kernel(*refs, own, rows):
    pair_refs, row_ref, out_ref = refs[:-2], refs[-2], refs[-1]
    reach = 2 * REACH + 1
    lane = lax.broadcasted_iota(jnp.int32, (GRID, own), 1)
    query_row, query_col = lane // GRID, lane % GRID
    col_diff = lax.broadcasted_iota(jnp.int32, (GRID, own), 0) - query_col
    zero = jnp.zeros((GRID, own), jnp.float32)
    for head in range(out_ref.shape[0]):
        by_row = [zero] * reach
        for b in range(rows):
            block = sum(pairs[head, b * GRID : (b + 1) * GRID, :] for pairs in pair_refs)
            row_diff = row_ref[b] - query_row
            for n in range(reach):
                by_row[n] = by_row[n] + jnp.where(row_diff == n - REACH, block, zero)
        for n in range(reach):
            for o in range(reach):
                kept = jnp.where(col_diff == o - REACH, by_row[n], zero)
                out_ref[head, n * reach + o, :] = jnp.sum(kept, axis=0)


def bias_sum(pairs, key_rows, own_rows):
    reach = 2 * REACH + 1
    rows = key_rows.shape[0]
    own, total = own_rows * GRID, rows * GRID
    heads = 4
    block = pl.BlockSpec((heads, total, own), lambda h: (h, 0, 0))
    by_lane = pl.pallas_call(
        functools.partial(bias_sum_kernel, own=own, rows=rows),
        grid=(HEADS // heads,),
        in_specs=[block] * len(pairs) + [pl.BlockSpec(memory_space=pltpu.SMEM)],
        out_specs=pl.BlockSpec((heads, reach * reach, own), lambda h: (h, 0, 0)),
        out_shape=jax.ShapeDtypeStruct((HEADS, reach * reach, own), jnp.float32),
        name="bias_sum",
    )(*pairs, key_rows)
    return jnp.sum(by_lane, axis=-1).reshape(HEADS, reach, reach)


def attend_kernel(mixed_ref, table_ref, out_ref, acc_ref, *, own, total):
    def columns(part, low, high, count):
        block = mixed_ref[0, : count // GRID, 0, :, part * D + low : part * D + high]
        return block.reshape(count, high - low)

    for head in range(HEADS):
        low, high = head_window(head)
        query = columns(0, low, high, own) * head_mask(head, jnp.bfloat16)
        scores = nt_dot(columns(1, low, high, total), query) * score_scale + table_ref[head]
        top = jnp.max(scores, axis=0, keepdims=True)
        weight = jnp.exp(scores - top)
        weight = weight * (1.0 / jnp.sum(weight, axis=0, keepdims=True))
        result = tn_dot(weight.astype(jnp.bfloat16), columns(2, low, high, total))
        if head * HEAD_DIM % LANES == 0:
            acc_ref[:, low:high] = result
        else:
            mine = head_mask(head, jnp.float32)
            earlier = acc_ref[:, low : low + LANES]
            acc_ref[:, low : low + LANES] = jnp.where(mine[:, :LANES] > 0, result[:, :LANES], earlier)
            if high - low > LANES:
                acc_ref[:, low + LANES : high] = result[:, LANES:]
    out_ref[0, :, 0] = acc_ref[...].astype(jnp.bfloat16).reshape(own // GRID, GRID, D)


def attend_back_kernel(mixed_ref, grad_ref, table_ref, *refs, own, total):
    out_ref, bias_ref, unit_ref, q_ref, k_ref, v_ref = refs[-6:]

    @pl.when((pl.program_id(0) == 0) & (pl.program_id(1) == 0))
    def _():
        bias_ref[...] = jnp.zeros_like(bias_ref)

    def columns(part, low, high, count):
        block = mixed_ref[0, : count // GRID, 0, :, part * D + low : part * D + high]
        return block.reshape(count, high - low)

    def put(ref, low, high, value, fresh):
        if fresh:
            ref[:, low:high] = value
        else:
            ref[:, low : low + LANES] += value[:, :LANES]
            if high - low > LANES:
                ref[:, low + LANES : high] = value[:, LANES:]

    for head in range(HEADS):
        low, high = head_window(head)
        fresh = head * HEAD_DIM % LANES == 0
        keep = head_mask(head, jnp.bfloat16)
        query = columns(0, low, high, own) * keep
        grad = grad_ref[0, :, 0, :, low:high].reshape(own, high - low) * keep
        keys = columns(1, low, high, total)
        scores = nt_dot(keys, query) * score_scale + table_ref[head]
        top = jnp.max(scores, axis=0, keepdims=True)
        weight = jnp.exp(scores - top)
        weight = weight * (1.0 / jnp.sum(weight, axis=0, keepdims=True))
        grad_weight = nt_dot(columns(2, low, high, total), grad)
        delta = jnp.sum(weight * grad_weight, axis=0, keepdims=True)
        grad_scores = weight * (grad_weight - delta)
        bias_ref[head] += grad_scores
        grad_low = grad_scores.astype(jnp.bfloat16)
        put(v_ref, low, high, low_dot(weight.astype(jnp.bfloat16), grad), fresh)
        put(k_ref, low, high, low_dot(grad_low, query), fresh)
        put(q_ref, low, high, tn_dot(grad_low, keys) * head_mask(head, jnp.float32), fresh)
    rows, own_rows = total // GRID, own // GRID
    out_ref[0, :own_rows, 0, :, :D] = (q_ref[...] * score_scale).astype(jnp.bfloat16).reshape(own_rows, GRID, D)
    if rows > own_rows:
        out_ref[0, own_rows:, 0, :, :D] = jnp.zeros((rows - own_rows, GRID, D), jnp.bfloat16)
    out_ref[0, :, 0, :, D : 2 * D] = (k_ref[...] * score_scale).astype(jnp.bfloat16).reshape(rows, GRID, D)
    out_ref[0, :, 0, :, 2 * D :] = v_ref[...].astype(jnp.bfloat16).reshape(rows, GRID, D)
    slot_at = pl.program_id(1)
    for part, ref, scale in ((0, q_ref, score_scale), (1, k_ref, score_scale), (2, v_ref, 1.0)):
        low = (ref[...] * scale).astype(jnp.bfloat16).astype(jnp.float32)
        unit_ref[0, pl.ds(slot_at, 1), part * D : (part + 1) * D] = jnp.sum(low, axis=0, keepdims=True)


def attend(mixed, table, own_rows):
    seqs, rows = mixed.shape[:2]
    own, total = own_rows * GRID, rows * GRID
    return pl.pallas_call(
        functools.partial(attend_kernel, own=own, total=total),
        grid=(seqs, PACK),
        in_specs=[
            pl.BlockSpec((1, rows, 1, GRID, 3 * D), lambda s, p: (s, 0, p, 0, 0)),
            pl.BlockSpec((HEADS, total, own), lambda s, p: (0, 0, 0)),
        ],
        out_specs=pl.BlockSpec((1, own_rows, 1, GRID, D), lambda s, p: (s, 0, p, 0, 0)),
        out_shape=jax.ShapeDtypeStruct((seqs, own_rows, PACK, GRID, D), jnp.bfloat16),
        scratch_shapes=[pltpu.VMEM((own, D), jnp.float32)],
        compiler_params=pltpu.CompilerParams(
            dimension_semantics=("arbitrary", "arbitrary"), vmem_limit_bytes=48 << 20
        ),
        name="attend",
    )(mixed, table)


def attend_back(mixed, grad, table, kept, span, own_rows):
    seqs, rows = mixed.shape[:2]
    own, total = own_rows * GRID, rows * GRID
    first = span.start
    kept = () if kept is None else (kept,)
    return pl.pallas_call(
        functools.partial(attend_back_kernel, own=own, total=total),
        grid=(span.stop - span.start, PACK),
        in_specs=[
            pl.BlockSpec((1, rows, 1, GRID, 3 * D), lambda s, p: (first + s, 0, p, 0, 0)),
            pl.BlockSpec((1, own_rows, 1, GRID, D), lambda s, p: (first + s, 0, p, 0, 0)),
            pl.BlockSpec((HEADS, total, own), lambda s, p: (0, 0, 0)),
        ]
        + [pl.BlockSpec(memory_space=pl.ANY)] * len(kept),
        out_specs=[
            pl.BlockSpec((1, rows, 1, GRID, 3 * D), lambda s, p: (first + s, 0, p, 0, 0)),
            pl.BlockSpec((HEADS, total, own), lambda s, p: (0, 0, 0)),
            pl.BlockSpec((1, PACK, 3 * D), lambda s, p: (s, 0, 0)),
        ],
        out_shape=[
            jax.ShapeDtypeStruct((seqs, rows, PACK, GRID, 3 * D), jnp.bfloat16),
            jax.ShapeDtypeStruct((HEADS, total, own), jnp.float32),
            jax.ShapeDtypeStruct((span.stop - span.start, PACK, 3 * D), jnp.float32),
        ],
        scratch_shapes=[
            pltpu.VMEM((own, D), jnp.float32),
            pltpu.VMEM((total, D), jnp.float32),
            pltpu.VMEM((total, D), jnp.float32),
        ],
        input_output_aliases={3: 0} if kept else {},
        compiler_params=pltpu.CompilerParams(
            dimension_semantics=("arbitrary", "arbitrary"), vmem_limit_bytes=48 << 20
        ),
        name="attend_back",
    )(mixed, grad, table, *kept)


def trade(block, axis, bit):
    size = lax.axis_size(axis)
    return lax.ppermute(block, axis, [(i, i ^ bit) for i in range(size)])


def gather_small(block):
    size = lax.axis_size("seq")
    place = lax.axis_index("seq")
    axis, bit = 0, size // 2
    while bit:
        got = trade(block, "seq", bit)
        upper = (place & bit) > 0
        block = jnp.stack([jnp.where(upper, got, block), jnp.where(upper, block, got)], axis=axis)
        axis, bit = axis + 1, bit // 2
    return block.reshape((size,) + block.shape[axis:])


def scatter_small(block):
    size = lax.axis_size("seq")
    place = lax.axis_index("seq")
    bit = 1
    while bit < size:
        block = block.reshape((block.shape[0] // 2, 2) + block.shape[1:])
        upper = (place & bit) > 0
        kept = jnp.where(upper, block[:, 1], block[:, 0])
        sent = jnp.where(upper, block[:, 0], block[:, 1])
        block = kept + trade(sent, "seq", bit)
        bit *= 2
    return block[0]


def after(value, *earlier):
    return lax.optimization_barrier((value,) + earlier)[0]


def ring_order(chips):
    return list(range(0, chips, 2)) + list(range(1, chips, 2))[::-1]


def ring_path(chips, step):
    order = ring_order(chips)
    return [(2 * order[i] + c, 2 * order[(i + step) % chips] + c) for i in range(chips) for c in range(2)]


def ring_spot(chips, chip):
    return jnp.where(chip % 2 == 0, chip // 2, chips - 1 - chip // 2)


def chip_at(chips, spot):
    spot = (spot + chips) % chips
    return jnp.where(spot < chips // 2, 2 * spot, 2 * chips - 1 - 2 * spot)


class RingGather:
    def __init__(self, shard):
        self.size = lax.axis_size("seq")
        self.chips = self.size // 2
        place = lax.axis_index("seq")
        self.core, self.chip = place % 2, place // 2
        self.spot = ring_spot(self.chips, self.chip)
        ahead = self.chips // 2
        self.hops = {1: ahead, -1: self.chips - 1 - ahead}
        self.moving = {1: shard, -1: shard}
        self.done = 0
        self.fresh = [(shard, self.chip)]
        self.pieces, self.at = [], []
        self.full = None

    def place_pieces(self):
        self.full = assemble(self.pieces, jnp.stack(self.at).astype(jnp.int32), self.size, self.full)
        self.pieces, self.at = [], []

    def steps(self):
        return [step for step in (1, -1) if self.done < self.hops[step]]

    def load(self):
        return tuple(self.moving[step] for step in self.steps()) + tuple(piece for piece, _ in self.fresh)

    def fly(self, loads):
        steps = self.steps()
        gots = tuple(
            lax.ppermute(block, "seq", ring_path(self.chips, step)) for block, step in zip(loads, steps)
        )
        return gots + tuple(trade(block, "seq", 1) for block in loads[len(steps) :])

    def land(self, loads, gots):
        steps = self.steps()
        self.done += 1
        for (piece, chip), other in zip(self.fresh, gots[len(steps) :]):
            self.pieces += [piece, other]
            self.at += [chip * 2 + self.core, chip * 2 + 1 - self.core]
        self.fresh = []
        for step, got in zip(steps, gots):
            self.moving[step] = got
            self.fresh.append((got, chip_at(self.chips, self.spot - step * self.done)))

    def whole(self):
        while self.fresh:
            slot([self], lambda: ())
        self.place_pieces()
        return self.full.reshape(-1, self.full.shape[-1])


class RingScatter:
    def __init__(self, *grads):
        self.size = lax.axis_size("seq")
        self.chips = self.size // 2
        place = lax.axis_index("seq")
        core, chip = place % 2, place // 2
        self.spot = ring_spot(self.chips, chip)
        self.widths = [grad.shape[1] for grad in grads]
        lows = [grad.astype(jnp.bfloat16).reshape(self.chips, 2, grad.shape[0] // self.size, -1) for grad in grads]

        def side(which):
            parts = [lax.dynamic_index_in_dim(low, which, 1, keepdims=False) for low in lows]
            return jnp.concatenate(parts, axis=-1) if len(parts) > 1 else parts[0]

        self.kept, self.sent = side(core), side(1 - core)
        ahead = self.chips // 2
        self.hops = {1: ahead, -1: self.chips - 1 - ahead}
        self.stage = 0
        self.got = {}
        self.total = None

    def pending(self):
        return self.total is None

    def parts(self):
        ends = [sum(self.widths[:i]) for i in range(len(self.widths) + 1)]
        return tuple(self.total[:, first:last] for first, last in zip(ends, ends[1:]))

    def piece(self, offset):
        at = chip_at(self.chips, self.spot + offset)
        return lax.dynamic_index_in_dim(self.chip_sum, at, 0, keepdims=False).astype(jnp.float32)

    def steps(self):
        return [step for step in (1, -1) if self.stage <= self.hops[step]]

    def load(self):
        if self.stage == 0:
            return (self.sent,)
        if self.steps():
            loads = []
            for step in self.steps():
                moving = self.piece(step * (self.hops[step] - self.stage + 1))
                if self.stage > 1:
                    moving = moving + self.got[step].astype(jnp.float32)
                loads.append(moving.astype(jnp.bfloat16))
            return tuple(loads)
        total = self.piece(0)
        for got in self.got.values():
            total = total + got.astype(jnp.float32)
        return (total.astype(jnp.bfloat16),)

    def fly(self, loads):
        if self.stage == 0:
            return (trade(loads[0], "seq", 1),)
        if self.steps():
            return tuple(
                lax.ppermute(block, "seq", ring_path(self.chips, step)) for block, step in zip(loads, self.steps())
            )
        if lax.axis_size("rows") == 2:
            return (trade(loads[0], "rows", 1),)
        return (lax.psum(loads[0], "rows"),)

    def land(self, loads, gots):
        if self.stage == 0:
            both = self.kept.astype(jnp.float32) + gots[0].astype(jnp.float32)
            self.chip_sum = both.astype(jnp.bfloat16)
        elif self.steps():
            for step, got in zip(self.steps(), gots):
                self.got[step] = got
        else:
            self.total = gots[0].astype(jnp.float32)
            if lax.axis_size("rows") == 2:
                self.total = self.total + loads[0].astype(jnp.float32)
        self.stage += 1


class RowSum:
    def __init__(self, block):
        self.block = block
        self.total = None

    def pending(self):
        return self.total is None

    def load(self):
        return (self.block,)

    def fly(self, loads):
        if lax.axis_size("rows") == 2:
            return (trade(loads[0], "rows", 1),)
        return (lax.psum(loads[0], "rows"),)

    def land(self, loads, gots):
        self.total = gots[0].astype(jnp.float32)
        if lax.axis_size("rows") == 2:
            self.total = self.total + loads[0].astype(jnp.float32)


class AllSum:
    def __init__(self, block):
        self.block = block
        self.rounds = []
        for axis in ("seq", "rows"):
            bit = 1
            while bit < lax.axis_size(axis):
                self.rounds.append((axis, bit))
                bit *= 2

    def pending(self):
        return bool(self.rounds)

    def load(self):
        return (self.block,)

    def fly(self, loads):
        return (trade(loads[0], *self.rounds[0]),)

    def land(self, loads, gots):
        self.block = loads[0] + gots[0]
        self.rounds.pop(0)


class Chain:
    def __init__(self, block, follow):
        self.follow = follow
        self.start(block)

    def start(self, block):
        self.block = block
        self.axis, self.bit = 0, lax.axis_size("seq") // 2

    def pending(self):
        return self.block is not None

    def load(self):
        return (self.block,)

    def fly(self, loads):
        return (trade(loads[0], "seq", self.bit),)

    def land(self, loads, gots):
        upper = (lax.axis_index("seq") & self.bit) > 0
        ends = [jnp.where(upper, gots[0], loads[0]), jnp.where(upper, loads[0], gots[0])]
        self.block = jnp.stack(ends, axis=self.axis)
        self.axis, self.bit = self.axis + 1, self.bit // 2
        if self.bit == 0:
            shape = self.block.shape[self.axis :]
            following = self.follow(self.block.reshape((-1,) + shape[1:]))
            self.block = None
            if following is not None:
                self.start(following)


class ReturnRows:
    def __init__(self, own, borrowed, shards):
        self.own, self.borrowed, self.shards = own, borrowed.astype(jnp.bfloat16), shards
        self.total = None

    def pending(self):
        return self.total is None

    def load(self):
        return (self.borrowed,)

    def fly(self, loads):
        one_sided, turns, sent = row_plan(self.own.shape[1], self.shards)
        if one_sided:
            return (lax.ppermute(loads[0], "rows", [(0, 1), (1, 0)]),)
        gots = []
        for piece, turn in enumerate([-t for t in range(turns, 0, -1)] + list(range(1, turns + 1))):
            block = loads[0][:, piece * sent : (piece + 1) * sent]
            gots.append(lax.ppermute(block, "rows", route(self.shards, turn)))
        return tuple(gots)

    def land(self, loads, gots):
        rows, own = self.own.shape[1], self.own
        one_sided, turns, sent = row_plan(rows, self.shards)
        if one_sided:
            got = gots[0].astype(own.dtype)
            room = [(0, 0)] * own.ndim
            at_end, at_start = list(room), list(room)
            at_end[1], at_start[1] = (rows - sent, 0), (0, rows - sent)
            first = lax.axis_index("rows") == 0
            self.total = own + jnp.where(first, jnp.pad(got, at_end), jnp.pad(got, at_start))
            return
        for piece, got in enumerate(gots):
            span = slice(rows - sent, None) if piece < turns else slice(0, sent)
            own = own.at[:, span].add(got.astype(own.dtype))
        self.total = own


def in_rows(parts):
    flats = [part.reshape(-1) for part in parts]
    return jnp.concatenate([jnp.pad(flat, (0, -flat.size % D)).reshape(-1, D) for flat in flats], axis=0)


def from_rows(rows, parts):
    found, first = [], 0
    for part in parts:
        count = -(-part.size // D)
        found.append(rows[first : first + count].reshape(-1)[: part.size].reshape(part.shape))
        first += count
    return found


def slot(rings, work, *values, wait=()):
    loads = [ring.load() for ring in rings]
    held = lax.optimization_barrier(tuple(values) + sum(loads, ()))
    values, rest = held[: len(values)], held[len(values) :]
    gots = []
    for i, ring in enumerate(rings):
        loads[i], rest = rest[: len(loads[i])], rest[len(loads[i]) :]
        gots.append(ring.fly(loads[i]))
    results = tuple(work(*values))
    held = lax.optimization_barrier(results + tuple(wait) + sum(gots, ()))
    results, rest = held[: len(results)], held[len(results) + len(wait) :]
    for i, ring in enumerate(rings):
        got, rest = rest[: len(gots[i])], rest[len(gots[i]) :]
        ring.land(loads[i], got)
    return results + held[len(results) : len(results) + len(wait)]


def on_device(
    row_shards,
    tokens,
    image_ids,
    timestep,
    norm1_gain,
    norm1_shift,
    time_in_weight,
    time_in_bias,
    time_out_weight,
    time_out_bias,
    mix_weight,
    time_mix_weight,
    position_bias,
    proj_weight,
    proj_bias,
    norm2_gain,
    norm2_shift,
    up_weight,
    up_bias,
    down_weight,
    down_bias,
    cotangent,
):
    seq_rows, local_rows, columns, _ = tokens.shape
    act_tokens = tokens.reshape(seq_rows, local_rows, PACK, GRID, D)
    act_cot = cotangent.reshape(seq_rows, local_rows, PACK, GRID, D)
    token_count = seq_rows * local_rows * columns
    seqs = lax.axis_size("seq")
    place = lax.axis_index("seq")
    images = seqs * seq_rows * PACK
    width_part, freq_part = D // seqs, FREQ // seqs

    def my_part(array, part, axis):
        return lax.dynamic_slice_in_dim(array, place * part, part, axis=axis)

    full_first = lax.all_gather(jnp.concatenate([mix_weight, proj_weight], axis=1), "seq", axis=0, tiled=True)
    full_mix, full_proj = full_first[:, : 3 * D], full_first[:, 3 * D :]
    borrowed, borrowed_at, sent_rows = borrow_rows(act_tokens, row_shards)
    timestep, time_in_weight = lax.optimization_barrier((timestep, time_in_weight, sent_rows))[:2]
    half_width = FREQ // 2
    frequency = jnp.exp(-math.log(10000.0) * jnp.arange(half_width, dtype=jnp.float32) / half_width)

    def time_first(timestep, time_in_weight):
        angles = timestep.astype(jnp.float32).reshape(-1, 1) * frequency
        features = jnp.concatenate([jnp.cos(angles), jnp.sin(angles)], axis=-1).astype(jnp.bfloat16)
        spare = -features.size % D
        features = jnp.pad(features.reshape(-1), (0, spare)).reshape(-1, D)
        both = gather_small(jnp.concatenate([time_in_weight, features], axis=0))
        full_tin = both[:, :freq_part].reshape(FREQ, D)
        features = both[:, freq_part:].reshape(seqs, -1)[:, : seq_rows * PACK * FREQ].reshape(images, FREQ)
        time_pre = jnp.einsum(
            "fd,if->di", my_part(full_tin, width_part, 1), features, preferred_element_type=jnp.float32
        )
        return (features, time_pre + my_part(time_in_bias, width_part, 0)[:, None])

    def time_second(time_pre):
        time_hidden = jax.nn.silu(time_pre).astype(jnp.bfloat16)
        partial = jnp.einsum("fd,fi->di", time_out_weight, time_hidden, preferred_element_type=jnp.float32)
        time_embed = scatter_small(partial.reshape(seqs, width_part, images))
        time_embed = time_embed + my_part(time_out_bias, width_part, 0)[:, None]
        return (time_hidden, time_embed.astype(jnp.bfloat16))

    def time_third(time_embed):
        partial = jnp.einsum("di,de->ie", time_embed, time_mix_weight, preferred_element_type=jnp.float32)
        return (scatter_small(partial.reshape(seqs, seq_rows * PACK, 3 * D)),)

    features, time_pre = time_first(timestep, time_in_weight)
    time_hidden, time_embed = time_second(time_pre)
    key_at = jnp.concatenate([jnp.arange(local_rows), borrowed_at])
    key_row = lax.axis_index("rows") * local_rows + key_at
    key_rows = jnp.where((key_row >= 0) & (key_row < GRID), key_at, 4 * GRID).astype(jnp.int32)
    table = bias_table(position_bias, key_rows, local_rows)
    time_embed = after(time_embed, table)
    (time_proj,) = time_third(time_embed)
    time_proj = time_proj.reshape(seq_rows, PACK, 3 * D)
    my_features = my_part(features, freq_part, 1)
    block_slots = image_ids[:, ::GRID]
    slot_hot = (block_slots[:, :, None] == jnp.arange(PACK, dtype=jnp.int32)[None, None, :]).astype(
        jnp.float32
    )
    unit_time = jnp.einsum("skp,spe->ske", slot_hot, time_proj, precision=highest)
    ext_tokens = jnp.concatenate([act_tokens, borrowed], axis=1)
    ext_rows = ext_tokens.shape[1]
    ext_count = seq_rows * ext_rows * columns

    normed1 = norm_forward(ext_tokens.astype(jnp.float32), norm1_gain, norm1_shift)[0].astype(jnp.bfloat16)
    full_up = lax.all_gather(up_weight, "seq", axis=0, tiled=True)
    down_ring = RingGather(after(down_weight, full_first[:8, :128]))

    def to_mixed(normed1):
        return ((low_dot(normed1, full_mix) + unit_time[:, None, :, None, :]).astype(jnp.bfloat16),)

    (mixed,) = slot([down_ring], to_mixed, normed1)
    (attended,) = slot([down_ring], lambda mixed: (attend(mixed, table, local_rows),), mixed)
    flat_tokens = act_tokens.astype(jnp.float32)

    def second_norm(attended):
        residual = flat_tokens + low_dot(attended, full_proj) + proj_bias
        normed2, unit_two, inverse_two = norm_forward(residual, norm2_gain, norm2_shift)
        return (residual, normed2.astype(jnp.bfloat16), unit_two, inverse_two)

    down_ring.place_pieces()
    attended = after(attended, down_ring.full)
    residual, normed2, unit_two, inverse_two = slot([down_ring], second_norm, attended)

    def to_hidden(normed2):
        pre = low_dot(normed2, full_up) + up_bias
        slope = math.sqrt(2.0 / math.pi)
        square = pre * pre
        bend = jnp.tanh(slope * pre * (1.0 + 0.044715 * square))
        half = 0.5 * (1.0 + bend)
        gelu_slope = half + 0.5 * pre * (1.0 - bend * bend) * (slope * (1.0 + 3.0 * 0.044715 * square))
        return ((pre * half).astype(jnp.bfloat16), gelu_slope.astype(jnp.bfloat16))

    hidden, gelu_slope = slot([down_ring], to_hidden, normed2)
    flat_hidden = hidden.reshape(token_count, FF)
    flat_cot = act_cot.reshape(token_count, D)

    def weight_down(flat_hidden):
        grad = jnp.einsum("nf,nd->fd", flat_hidden, flat_cot, preferred_element_type=jnp.float32)
        return (grad.astype(jnp.bfloat16),)

    (grad_down_w,) = slot([down_ring], weight_down, flat_hidden)
    full_down = down_ring.whole()
    grad_down_b = jnp.sum(flat_cot, axis=0, dtype=jnp.float32)
    down_part = lax.psum_scatter(grad_down_w, "seq", scatter_dimension=0, tiled=True)
    grad_hidden = jnp.einsum(
        "nd,fd->nf", flat_cot, full_down, preferred_element_type=jnp.float32
    )
    grad_pre = (grad_hidden * gelu_slope.reshape(token_count, FF).astype(jnp.float32)).astype(jnp.bfloat16)
    flat_normed2 = normed2.reshape(token_count, D)
    grad_up_w = jnp.einsum("nd,nf->df", flat_normed2, grad_pre, preferred_element_type=jnp.float32)
    grad_up_b = jnp.sum(grad_pre, axis=0, dtype=jnp.float32)
    def back_up(grad_pre):
        grad_normed2 = jnp.einsum("nf,df->nd", grad_pre, full_up, preferred_element_type=jnp.float32)
        return (grad_normed2.reshape(act_tokens.shape),)

    def back_norm(grad_normed2):
        grad_norm_two, grad_gain_two, grad_shift_two = norm_backward(
            grad_normed2, unit_two, inverse_two, norm2_gain
        )
        grad_residual = act_cot.astype(jnp.float32) + grad_norm_two
        grad_branch = grad_residual.astype(jnp.bfloat16).reshape(token_count, D)
        grad_proj_w = jnp.einsum(
            "nd,ne->de", attended.reshape(token_count, D), grad_branch, preferred_element_type=jnp.float32
        ).astype(jnp.bfloat16)
        grad_proj_b = jnp.sum(grad_branch, axis=0, dtype=jnp.float32)
        grad_attended = jnp.einsum(
            "ne,de->nd", grad_branch, full_proj, preferred_element_type=jnp.float32
        ).astype(jnp.bfloat16)
        grad_attended = grad_attended.reshape(act_tokens.shape)
        return (grad_residual, grad_gain_two, grad_shift_two, grad_proj_w, grad_proj_b, grad_attended)

    grad_up_w = grad_up_w.astype(jnp.bfloat16)
    (grad_normed2,) = back_up(grad_pre)
    up_sum = RingScatter(grad_up_w)
    (grad_residual, grad_gain_two, grad_shift_two, grad_proj_w, grad_proj_b, grad_attended) = slot(
        [up_sum], back_norm, grad_normed2
    )
    proj_part = lax.psum_scatter(grad_proj_w, "seq", scatter_dimension=0, tiled=True)
    part = -(-seq_rows // 2)
    spans = [slice(0, part), slice(part, seq_rows)][: min(2, seq_rows)]
    grad_mixed, grad_tables, grad_units = None, [], []
    for span in spans:
        held = (grad_attended,) if grad_mixed is None else (grad_attended, grad_mixed)
        grad_mixed, grad_table, grad_unit = slot(
            [up_sum], lambda grad, kept=None: attend_back(mixed, grad, table, kept, span, local_rows), *held
        )
        grad_tables.append(grad_table)
        grad_units.append(grad_unit)
    grad_unit = jnp.concatenate(grad_units, axis=0)
    unit_sum, down_sum = RowSum(grad_unit), RowSum(down_part)

    def weight_mix(grad_mixed):
        grad_mix_w = jnp.einsum(
            "nd,ne->de",
            normed1.reshape(ext_count, D),
            grad_mixed.reshape(ext_count, 3 * D),
            preferred_element_type=jnp.float32,
        )
        return (grad_mix_w.astype(jnp.bfloat16),)

    (grad_mix_w,) = slot([unit_sum, up_sum, down_sum], weight_mix, grad_mixed)
    found = {}

    def from_time_proj(gathered):
        found["tmix"] = low_dot(time_embed, gathered)
        grad_embed = jnp.einsum("de,ie->di", time_mix_weight, gathered, preferred_element_type=jnp.float32)
        chain.follow = from_embed
        return grad_embed.astype(jnp.bfloat16)

    def from_embed(gathered):
        found["tout"] = jnp.einsum("fi,di->fd", time_hidden, gathered, preferred_element_type=jnp.float32)
        found["tout_b"] = jnp.sum(gathered, axis=1, dtype=jnp.float32)
        silu_back = jax.vjp(jax.nn.silu, time_pre)[1]
        chain.follow = from_pre
        return silu_back(low_dot(time_out_weight, gathered))[0].astype(jnp.bfloat16)

    def from_pre(gathered):
        found["tin"] = jnp.einsum("if,di->fd", my_features, gathered, preferred_element_type=jnp.float32)
        found["tin_b"] = jnp.sum(gathered, axis=1, dtype=jnp.float32)

    grad_time_proj = jnp.einsum("skp,ske->spe", slot_hot, unit_sum.total, precision=highest)
    chain = Chain(grad_time_proj.astype(jnp.bfloat16).reshape(-1, 3 * D), from_time_proj)
    mix_part = lax.psum_scatter(grad_mix_w, "seq", scatter_dimension=0, tiled=True)
    first_sums = (grad_proj_b, grad_gain_two, grad_shift_two, grad_up_b, grad_down_b)
    rings = [up_sum, chain]

    def run(work, *values):
        return slot([ring for ring in rings if ring.pending()], work, *values)

    def back_mixed(grad_mixed, span):
        rows = grad_mixed[span]
        grad_in = jnp.einsum("spcge,de->spcgd", rows, full_mix, preferred_element_type=jnp.float32)
        return (grad_in[:, :local_rows], grad_in[:, local_rows:].astype(jnp.bfloat16))

    def back_first(grad_normed1, tokens, grad_residual, span):
        _, unit_one, inverse_one = norm_forward(tokens[span].astype(jnp.float32), norm1_gain, norm1_shift)
        grad_norm_one, gain, shift = norm_backward(grad_normed1, unit_one, inverse_one, norm1_gain)
        return ((grad_residual[span] + grad_norm_one).astype(jnp.bfloat16), gain, shift)

    def last_part(hidden, residual, span):
        return ((residual[span] + low_dot(hidden[span], full_down) + down_bias).astype(jnp.bfloat16),)

    (bias_grad,) = run(lambda *pairs: (bias_sum(pairs, key_rows, local_rows),), *grad_tables)
    returned = []
    for span in spans:
        returned.append(ReturnRows(*run(functools.partial(back_mixed, span=span), grad_mixed), row_shards))
        rings.append(returned[-1])
    outputs, tokens_grads, firsts = [], [], []

    def finish(span):
        outputs.extend(run(functools.partial(last_part, span=span), hidden, residual))

    finish(spans[0])
    for span, back in zip(spans, returned):
        firsts.append(run(functools.partial(back_first, span=span), back.total, act_tokens, grad_residual))
        tokens_grads.append(firsts[-1][0])
    grad_gain_one, grad_shift_one = (sum(part) for part in zip(*[first[1:] for first in firsts]))
    late_sums = (grad_gain_one, grad_shift_one, bias_grad) + first_sums
    late_sum = AllSum(in_rows(late_sums))
    proj_sum, mix_sum = RowSum(proj_part), RowSum(mix_part)
    rings += [late_sum, proj_sum]
    for span in spans[1:]:
        finish(span)
    output = jnp.concatenate(outputs, axis=0)
    tokens_grad = jnp.concatenate(tokens_grads, axis=0)
    while any(ring.pending() for ring in rings):
        run(lambda: ())
    slot([mix_sum], lambda: ())

    (gain_one, shift_one, bias_total, proj_total, gain_two, shift_two, up_total, down_total) = from_rows(
        late_sum.block, late_sums
    )
    sum_down, sum_up, sum_mix, sum_proj = down_sum.total, up_sum.total, mix_sum.total, proj_sum.total
    sum_tmix, sum_tout, sum_tin = found["tmix"], found["tout"], found["tin"]
    tout_bias, tin_bias = found["tout_b"], found["tin_b"]
    output = output.reshape(tokens.shape)
    tokens_grad = tokens_grad.reshape(tokens.shape)
    return (
        output,
        tokens_grad,
        gain_one,
        shift_one,
        sum_tin,
        tin_bias,
        sum_tout,
        tout_bias,
        sum_mix,
        sum_tmix,
        bias_total,
        sum_proj,
        proj_total,
        gain_two,
        shift_two,
        sum_up,
        up_total,
        sum_down,
        down_total,
    )


def solution(mesh):
    whole, sharded = (P(), P("seq", None))
    acts = P("seq", "rows", None, None)
    return jax.shard_map(
        functools.partial(on_device, mesh.shape["rows"]),
        mesh=mesh,
        in_specs=(
            acts,
            sharded,
            sharded,
            whole,
            whole,
            sharded,
            whole,
            sharded,
            whole,
            sharded,
            sharded,
            whole,
            sharded,
            whole,
            whole,
            whole,
            sharded,
            whole,
            sharded,
            whole,
            acts,
        ),
        out_specs=(
            acts,
            acts,
            whole,
            whole,
            sharded,
            whole,
            sharded,
            whole,
            sharded,
            sharded,
            whole,
            sharded,
            whole,
            whole,
            whole,
            sharded,
            whole,
            sharded,
            whole,
        ),
        check_vma=False,
    )
```

profile of v0, /device:TPU:0, one launch (start us, length us, event | category | flops | bytes accessed | tf_op | source)
XLA Modules:
  0.0 633.0 jit_solution(13265654229808528102)
XLA Ops:
  9.4 2.4 constant_dynamic-slice_fusion
  12.1 4.1 collective-permute-start.1
  16.2 2.7 collective-permute-done.1
  20.4 3.4 collective-permute-done.2
  25.7 9.5 %collective-permute-done.3 = bf16[2,2,18,1152]{3,2,0,1:T(8,128)(2,1)S(1)} collective-permute-done((bf16[2,2,18,1152]{3,2,0,1:T(8,128)(2,1)S(1)}, bf16[2,2,18,1152]{3,2,0,1:T(8,128)(2,1)S(1)}, u32[]{:S(2)}, u32[]{:S(2)}) %collective-permute-start.3) | collective-permute-done | bytes 165920 | tf_op jit(solution)/shard_map/ppermute | solution.py:341
  45.4 2.7 collective-permute-done.6
  49.8 2.7 collective-permute-done.7
  52.6 3.4 collective-permute-start.8
  58.2 6.9 %bias_table.1.table_ref = f32[16,192,128]{2,1,0:T(8,128)} custom-call(f32[16,81]{1,0:T(8,128)} %reshape.540.bias_ref, s32[12]{0:T(128)} %and_select_fusion.row_ref.refs_2_), custom_call_target="tpu_custom_call" | custom-call | tf_op jit(solution)/shard_map/bias_table/pallas_call | solution.py:125
  68.5 3.2 collective-permute-done
  75.6 2.5 fusion.16
  78.1 14.5 %collective-permute-done.10 = f32[4,8,3456]{2,1,0:T(8,128)S(1)} collective-permute-done((f32[4,8,3456]{2,1,0:T(8,128)S(1)}, f32[4,8,3456]{2,1,0:T(8,128)S(1)}, u32[]{:S(2)}, u32[]{:S(2)}) %collective-permute-start.10) | collective-permute-done | bytes 442400 | tf_op jit(solution)/shard_map/ppermute | solution.py:341
  94.3 15.6 %collective-permute-done.11 = f32[2,8,3456]{2,1,0:T(8,128)S(1)} collective-permute-done((f32[2,8,3456]{2,1,0:T(8,128)S(1)}, f32[2,8,3456]{2,1,0:T(8,128)S(1)}, u32[]{:S(2)}, u32[]{:S(2)}) %collective-permute-start.11) | collective-permute-done | bytes 221216 | tf_op jit(solution)/shard_map/ppermute | solution.py:341
  110.6 3.9 fusion.19
  114.5 2.3 collective-permute-start.13
  118.2 20.6 %add_convert_fusion.mixed_ref = bf16[2,12,4,16,3456]{4,3,2,1,0:T(8,128)(2,1)} fusion(f32[2,4,3456]{2,1,0:T(4,128)S(1)} %fusion.124, bf16[2,12,4,16,1152]{4,3,2,1,0:T(8,128)(2,1)} %fusion.19, bf16[1152,4608]{1,0:T(8,128)(2,1)} %all-gather.3.cloned.1.call-done), kind=kOutput, calls=%fused_computation | convolution fusion | flops 12241207296 | bytes 22228992 | tf_op jit(solution)/shard_map/dot_general | solution.py:29
  140.2 13.4 %collective-permute-done.14.refs_4_ = bf16[288,1152]{1,0:T(8,128)(2,1)} collective-permute-done((bf16[288,1152]{1,0:T(8,128)(2,1)S(1)}, bf16[288,1152]{1,0:T(8,128)(2,1)}, u32[]{:S(2)}, u32[]{:S(2)}) %collective-permute-start.14) | collective-permute-done | bytes 663584 | tf_op jit(solution)/shard_map/ppermute | solution.py:420
  153.6 2.2 collective-permute-start.17
  156.5 27.9 %attend.1 = bf16[2,8,4,16,1152]{4,3,2,1,0:T(8,128)(2,1)S(1)} custom-call(bf16[2,12,4,16,3456]{4,3,2,1,0:T(8,128)(2,1)} %add_convert_fusion.mixed_ref, f32[16,192,128]{2,1,0:T(8,128)S(1)} %copy-done.1), custom_call_target="tpu_custom_call" | custom-call | tf_op jit(solution)/shard_map/attend/pallas_call | solution.py:285
  184.5 4.7 assemble.2.refs_10_
  191.8 5.5 fusion.132
  199.2 3.8 add_convert_fusion.2
  203.0 15.5 %collective-permute-done.20.refs_4_ = bf16[288,1152]{1,0:T(8,128)(2,1)S(1)} collective-permute-done((bf16[288,1152]{1,0:T(8,128)(2,1)S(1)}, bf16[288,1152]{1,0:T(8,128)(2,1)S(1)}, u32[]{:S(2)}, u32[]{:S(2)}) %collective-permute-start.20) | collective-permute-done | bytes 663584 | tf_op jit(solution)/shard_map/ppermute | solution.py:420
  218.5 7.2 %collective-permute-done.21.refs_6_ = bf16[288,1152]{1,0:T(8,128)(2,1)} collective-permute-done((bf16[288,1152]{1,0:T(8,128)(2,1)}, bf16[288,1152]{1,0:T(8,128)(2,1)}, u32[]{:S(2)}, u32[]{:S(2)}) %collective-permute-start.21) | collective-permute-done | bytes 663584 | tf_op jit(solution)/shard_map/ppermute | solution.py:420
  228.8 26.2 %add_convert_fusion.1 = (bf16[2,8,4,16,4608]{4,3,2,1,0:T(8,128)(2,1)}, bf16[2,8,4,16,4608]{4,3,2,1,0:T(8,128)(2,1)S(1)}) fusion(f32[4608]{0:T(1024)S(1)} %copy-done.61, bf16[2,8,4,16,1152]{4,3,2,1,0:T(8,128)(2,1)} %get-tuple-element.208, bf16[1152,4608]{1,0:T(8,128)(2,1)} %all-gather.5.cloned.1.call-done), kind=kOutput, calls=%fused_computation.6 | convolution fusion | flops 10966007808 | bytes 31868928 | tf_op jit(solution)/shard_map/dot_general | solution.py:29
  255.1 3.5 copy-done.64
  258.6 14.8 %convolution_convert_fusion.1 = bf16[4608,1152]{1,0:T(8,128)(2,1)} fusion(bf16[1024,4608]{1,0:T(8,128)(2,1)S(1)} %bitcast.486, bf16[1024,1152]{1,0:T(8,128)(2,1)S(1)} %bitcast.460), kind=kOutput, calls=%fused_computation.2 | convolution fusion | flops 10876944384 | bytes 22413312 | tf_op jit(solution)/shard_map/nf,nd->fd/dot_general | solution.py:784
  275.9 6.4 %assemble.3 = bf16[16,288,1152]{2,1,0:T(8,128)(2,1)} custom-call(s32[10]{0:T(128)S(1)} %stack.227.at_ref, bf16[288,1152]{1,0:T(8,128)(2,1)S(1)} %collective-permute-done.16.refs_0_, bf16[288,1152]{1,0:T(8,128)(2,1)S(1)} %copy-done.12, bf16[288,1152]{1,0:T(8,128)(2,1)} %collective-permute-done.17.refs_2_, ...), custom_call_target="tpu_custom_call", output_to_operand_aliasing={{}: (11, {})} | custom-call | tf_op jit(solution)/shard_map/assemble/pallas_call | solution.py:151
  282.3 22.0 %convert_reduce_fusion = (f32[4608]{0:T(1024)}, bf16[1024,4608]{1,0:T(8,128)(2,1)}) fusion(bf16[2,8,4,16,4608]{4,3,2,1,0:T(8,128)(2,1)} %get-tuple-element.223, bf16[4608,1152]{1,0:T(8,128)(2,1)} %bitcast.445, bf16[1024,1152]{1,0:T(8,128)(2,1)S(1)} %bitcast.461), kind=kOutput, calls=%fused_computation.5 | convolution fusion | flops 10895224832 | bytes 31868928 | tf_op jit(solution)/shard_map/nd,fd->nf/dot_general | solution.py:791
  304.3 14.8 %convolution_convert_fusion = bf16[1152,4608]{1,0:T(8,128)(2,1)S(1)} fusion(bf16[1024,1152]{1,0:T(8,128)(2,1)S(1)} %bitcast.475, bf16[1024,4608]{1,0:T(8,128)(2,1)} %get-tuple-element.432), kind=kOutput, calls=%fused_computation.1 | convolution fusion | flops 10876944384 | bytes 22413312 | tf_op jit(solution)/shard_map/nd,nf->df/dot_general | solution.py:796
  319.1 4.0 copy-done.23
  323.1 2.7 dynamic-slice_bitcast_fusion
  325.8 16.1 %fusion.134 = f32[1024,1152]{1,0:T(8,128)S(1)} fusion(bf16[1024,4608]{1,0:T(8,128)(2,1)} %get-tuple-element.432, bf16[1152,4608]{1,0:T(8,128)(2,1)} %all-gather.5.cloned.1.call-done), kind=kOutput, calls=%fused_computation.268 | convolution fusion | flops 10871635968 | bytes 24772608 | tf_op jit(solution)/shard_map/nf,df->nd/dot_general | solution.py:799
  342.1 2.6 multiply_reduce_fusion
  344.8 3.2 convert_reduce_fusion.2
  347.9 6.7 %convolution_convert_fusion.3 = bf16[1024,1152]{1,0:T(8,128)(2,1)} fusion(bf16[1024,1152]{1,0:T(8,128)(2,1)S(1)} %bitcast.476, bf16[1152,4608]{1,0:T(8,128)(2,1)} %all-gather.3.cloned.1.call-done), kind=kOutput, calls=%fused_computation.58 | convolution fusion | flops 2719088640 | bytes 7372800 | tf_op jit(solution)/shard_map/ne,de->nd/dot_general | solution.py:812
  354.6 4.9 fusion.15
  359.6 5.6 fusion.2
  365.2 2.3 copy-done.19
  372.3 23.0 %attend_back.2 = (bf16[2,12,4,16,3456]{4,3,2,1,0:T(8,128)(2,1)}, f32[16,192,128]{2,1,0:T(8,128)S(1)}, f32[1,4,3456]{2,1,0:T(4,128)S(1)}) custom-call(bf16[2,12,4,16,3456]{4,3,2,1,0:T(8,128)(2,1)} %add_convert_fusion.mixed_ref, bf16[2,8,4,16,1152]{4,3,2,1,0:T(8,128)(2,1)S(1)} %bitcast.430, f32[16,192,128]{2,1,0:T(8,128)S(1)} %copy-done.1), custom_call_target="tpu_custom_call" | custom-call | tf_op jit(solution)/shard_map/attend_back/pallas_call | solution.py:307
  398.4 7.2 %collective-permute-done.30 = bf16[72,4608]{1,0:T(8,128)(2,1)S(1)} collective-permute-done((bf16[72,4608]{1,0:T(8,128)(2,1)}, bf16[72,4608]{1,0:T(8,128)(2,1)S(1)}, u32[]{:S(2)}, u32[]{:S(2)}) %collective-permute-start.30) | collective-permute-done | bytes 663584 | tf_op jit(solution)/shard_map/ppermute | solution.py:498
  406.4 2.6 fusion.99
  412.8 22.4 %attend_back.3 = (bf16[2,12,4,16,3456]{4,3,2,1,0:T(8,128)(2,1)}, f32[16,192,128]{2,1,0:T(8,128)S(1)}, f32[1,4,3456]{2,1,0:T(4,128)S(1)}) custom-call(bf16[2,12,4,16,3456]{4,3,2,1,0:T(8,128)(2,1)} %add_convert_fusion.mixed_ref, bf16[2,8,4,16,1152]{4,3,2,1,0:T(8,128)(2,1)S(1)} %bitcast.431, ...), custom_call_target="tpu_custom_call", output_to_operand_aliasing={{0}: (3, {})} | custom-call | tf_op jit(solution)/shard_map/attend_back/pallas_call | solution.py:307
  437.0 2.6 fusion.94
  443.6 19.6 %fusion.1 = bf16[1152,3456]{1,0:T(8,128)(2,1)} fusion(bf16[2,12,4,16,1152]{4,3,2,1,0:T(8,128)(2,1)} %fusion.19, bf16[2,12,4,16,3456]{4,3,2,1,0:T(8,128)(2,1)} %get-tuple-element.272), kind=kOutput, calls=%fused_computation.11 | convolution fusion | flops 12234571776 | bytes 22118400 | tf_op jit(solution)/shard_map/nd,ne->de/dot_general | solution.py:839
  463.6 2.2 collective-permute-done.35
  469.1 2.3 fusion.96
  479.3 2.3 convert_add_fusion.7
  481.6 5.3 bias_sum.1
  489.2 3.3 collective-permute-done.38
  496.6 2.7 collective-permute-start.40
  499.3 11.1 %fusion.33 = f32[1,12,4,16,1152]{4,3,2,1,0:T(8,128)S(1)} fusion(bf16[1152,4608]{1,0:T(8,128)(2,1)} %all-gather.3.cloned.1.call-done, bf16[2,12,4,16,3456]{4,3,2,1,0:T(8,128)(2,1)} %get-tuple-element.272), kind=kOutput, calls=%fused_computation.56 | convolution fusion | flops 6115295232 | bytes 16809984 | tf_op jit(solution)/shard_map/spcge,de->spcgd/dot_general | solution.py:878
  515.5 3.1 collective-permute-start.41
  520.0 11.2 %fusion.38 = f32[1,12,4,16,1152]{4,3,2,1,0:T(8,128)S(1)} fusion(bf16[1152,4608]{1,0:T(8,128)(2,1)} %all-gather.3.cloned.1.call-done, bf16[2,12,4,16,3456]{4,3,2,1,0:T(8,128)(2,1)} %get-tuple-element.272), kind=kOutput, calls=%fused_computation.57 | convolution fusion | flops 6115295232 | bytes 16809984 | tf_op jit(solution)/shard_map/spcge,de->spcgd/dot_general | solution.py:878
  531.2 2.8 convert_add_fusion.8
  534.7 9.5 %fusion.64 = bf16[1,8,4,16,1152]{4,3,2,1,0:T(8,128)(2,1)} fusion(bf16[4608,1152,1,1]{1,0,3,2:T(8,128)(2,1)S(1)} %bitcast.449, bf16[2,8,4,16,4608]{4,3,2,1,0:T(8,128)(2,1)} %copy-done.64, f32[2,8,4,16,1152]{4,3,2,1,0:T(8,128)} %copy-done.20, f32[1152]{0:T(1024)S(1)} %copy-done.63), kind=kOutput, calls=%fused_computation.67 | convolution fusion | flops 5437587456 | bytes 18878976 | tf_op jit(solution)/shard_map/dot_general | solution.py:29
  544.3 5.7 collective-permute-done.44
  555.3 2.2 collective-permute-done.45
  564.0 12.0 %fusion.61 = bf16[1,8,4,16,1152]{4,3,2,1,0:T(8,128)(2,1)S(1)} fusion(bf16[4608,1152,1,1]{1,0,3,2:T(8,128)(2,1)} %bitcast.446, bf16[2,8,4,16,4608]{4,3,2,1,0:T(8,128)(2,1)} %copy-done.64, f32[2,8,4,16,1152]{4,3,2,1,0:T(8,128)} %copy-done.20, f32[1152]{0:T(1024)S(1)} %copy-done.63), kind=kOutput, calls=%fused_computation.66 | convolution fusion | flops 5437587456 | bytes 18878976 | tf_op jit(solution)/shard_map/dot_general | solution.py:29
  579.4 3.5 collective-permute-done.51
  588.8 5.4 collective-permute-done.53
  594.3 2.7 collective-permute-start.55
  613.7 10.2 %collective-permute-done.59 = bf16[72,3456]{1,0:T(8,128)(2,1)S(1)} collective-permute-done((bf16[72,3456]{1,0:T(8,128)(2,1)}, bf16[72,3456]{1,0:T(8,128)(2,1)S(1)}, u32[]{:S(2)}, u32[]{:S(2)}) %collective-permute-start.59) | collective-permute-done | bytes 497696 | tf_op jit(solution)/shard_map/ppermute | solution.py:341
  624.0 2.1 convert_add_fusion.9
  (421 shorter events, 123.7 us)
Async XLA Ops:
  7.2 111.0 %all-gather.3.cloned.1.call-start = ((), (), s32[]{:S(2)}) async-start(), calls=%async_computation.3 | async-start | bytes 11280384 | tf_op jit(solution)/shard_map/all_gather | solution.py:700
  9.3 219.4 %all-gather.5.cloned.1.call-start = ((), (), s32[]{:S(2)}) async-start(), calls=%async_computation.4 | async-start | bytes 11280384 | tf_op jit(solution)/shard_map/all_gather | solution.py:751
  12.1 6.8 %collective-permute-start.1 = (bf16[18,1152]{1,0:T(8,128)(2,1)S(1)}, bf16[18,1152]{1,0:T(8,128)(2,1)S(1)}, u32[]{:S(2)}, u32[]{:S(2)}) collective-permute-start(bf16[18,1152]{1,0:T(8,128)(2,1)S(1)} %constant_dynamic-update-slice_fusion), channel_id=1, source_target_pairs={{0,16},{2,18},{4,20},{6,22},{8,24},{10,26},{12,28},{14,30},{16,0},... | collective-permute-start | bytes 124424 | tf_op jit(solution)/shard_map/ppermute | solution.py:341
  19.0 4.8 collective-permute-start.2
  23.9 11.3 %collective-permute-start.3 = (bf16[2,2,18,1152]{3,2,0,1:T(8,128)(2,1)S(1)}, bf16[2,2,18,1152]{3,2,0,1:T(8,128)(2,1)S(1)}, u32[]{:S(2)}, u32[]{:S(2)}) collective-permute-start(bf16[2,2,18,1152]{3,2,0,1:T(8,128)(2,1)S(1)} %pad_maximum_fusion.10), channel_id=1, source_target_pairs={{0,4},{2,6},{4,0},{6,2},{8,12},{10,14},{12,8},{14,10},{16,20},{18,... | collective-permute-start | bytes 497672 | tf_op jit(solution)/shard_map/ppermute | solution.py:341
  35.4 1.9 collective-permute-start.4
  42.1 6.0 collective-permute-start.6
  43.6 28.0 %collective-permute-start = (bf16[2,4,4,16,1152]{4,3,2,1,0:T(8,128)(2,1)}, bf16[2,4,4,16,1152]{4,3,2,1,0:T(8,128)(2,1)}, u32[]{:S(2)}, u32[]{:S(2)}) collective-permute-start(bf16[2,4,4,16,1152]{4,3,2,1,0:T(8,128)(2,1)} %constant_dynamic-slice_fusion), channel_id=1, source_target_pairs={{0,1},{1,0},{2,3},{3,2},{4,5},{5,4},{6,7},{7,6},{8,9},{9,8},{10,11... | collective-permute-start | bytes 3538952 | tf_op jit(solution)/shard_map/ppermute | solution.py:68
  45.4 394.2 %reduce-scatter.8.cloned.1.call-start = ((), (), s32[]{:S(2)}) async-start(), calls=%async_computation.5 | async-start | bytes 11280384 | tf_op jit(solution)/shard_map/reduce_scatter | solution.py:790
  48.1 4.4 collective-permute-start.7
  52.6 12.4 %collective-permute-start.8 = (f32[1,72,128]{2,1,0:T(8,128)S(1)}, f32[1,72,128]{2,1,0:T(8,128)S(1)}, u32[]{:S(2)}, u32[]{:S(2)}) collective-permute-start(f32[1,72,128]{2,1,0:T(8,128)S(1)} %select_bitcast_fusion.35), channel_id=1, source_target_pairs={{0,16},{2,18},{4,20},{6,22},{8,24},{10,26},{12,28},{14,30},{16,0},... | collective-permute-start | bytes 110600 | tf_op jit(solution)/shard_map/ppermute | solution.py:341
  68.4 5.1 collective-permute-start.9
  74.9 17.7 %collective-permute-start.10 = (f32[4,8,3456]{2,1,0:T(8,128)S(1)}, f32[4,8,3456]{2,1,0:T(8,128)S(1)}, u32[]{:S(2)}, u32[]{:S(2)}) collective-permute-start(f32[4,8,3456]{2,1,0:T(8,128)S(1)} %select_bitcast_fusion.3), channel_id=1, source_target_pairs={{0,4},{2,6},{4,0},{6,2},{8,12},{10,14},{12,8},{14,10},{16,20},{18,... | collective-permute-start | bytes 1327112 | tf_op jit(solution)/shard_map/ppermute | solution.py:341
  92.7 17.2 %collective-permute-start.11 = (f32[2,8,3456]{2,1,0:T(8,128)S(1)}, f32[2,8,3456]{2,1,0:T(8,128)S(1)}, u32[]{:S(2)}, u32[]{:S(2)}) collective-permute-start(f32[2,8,3456]{2,1,0:T(8,128)S(1)} %select_bitcast_fusion.9), channel_id=1, source_target_pairs={{0,8},{2,10},{4,12},{6,14},{8,0},{10,2},{12,4},{14,6},{16,24},{18,... | collective-permute-start | bytes 663560 | tf_op jit(solution)/shard_map/ppermute | solution.py:341
  110.0 7.9 %collective-permute-start.12 = (f32[1,8,3456]{2,1,0:T(8,128)S(1)}, f32[1,8,3456]{2,1,0:T(8,128)S(1)}, u32[]{:S(2)}, u32[]{:S(2)}) collective-permute-start(f32[1,8,3456]{2,1,0:T(8,128)S(1)} %select_bitcast_fusion.19), channel_id=1, source_target_pairs={{0,16},{2,18},{4,20},{6,22},{8,24},{10,26},{12,28},{14,30},{16,0},... | collective-permute-start | bytes 331784 | tf_op jit(solution)/shard_map/ppermute | solution.py:341
  114.5 25.7 %collective-permute-start.13 = (bf16[288,1152]{1,0:T(8,128)(2,1)S(1)}, bf16[288,1152]{1,0:T(8,128)(2,1)S(1)}, u32[]{:S(2)}, u32[]{:S(2)}) collective-permute-start(bf16[288,1152]{1,0:T(8,128)(2,1)S(1)} %copy-done.8), channel_id=1, source_target_pairs={{0,8},{2,10},{8,16},{10,18},{16,24},{18,26},{24,28},{26,30},{28,20... | collective-permute-start | bytes 1990664 | tf_op jit(solution)/shard_map/ppermute | solution.py:420
  116.8 36.8 %collective-permute-start.14 = (bf16[288,1152]{1,0:T(8,128)(2,1)S(1)}, bf16[288,1152]{1,0:T(8,128)(2,1)}, u32[]{:S(2)}, u32[]{:S(2)}) collective-permute-start(bf16[288,1152]{1,0:T(8,128)(2,1)S(1)} %copy-done.8), channel_id=1, source_target_pairs={{0,4},{2,6},{8,0},{10,2},{16,8},{18,10},{24,16},{26,18},{28,24},{3... | collective-permute-start | bytes 1990664 | tf_op jit(solution)/shard_map/ppermute | solution.py:420
  116.8 36.8 %collective-permute-start.15 = (bf16[288,1152]{1,0:T(8,128)(2,1)S(1)}, bf16[288,1152]{1,0:T(8,128)(2,1)}, u32[]{:S(2)}, u32[]{:S(2)}) collective-permute-start(bf16[288,1152]{1,0:T(8,128)(2,1)S(1)} %copy-done.8), channel_id=1, source_target_pairs={{0,2},{2,0},{4,6},{6,4},{8,10},{10,8},{12,14},{14,12},{16,18},{18,... | collective-permute-start | bytes 1990664 | tf_op jit(solution)/shard_map/ppermute | solution.py:341
  153.6 30.8 %collective-permute-start.16 = (bf16[288,1152]{1,0:T(8,128)(2,1)}, bf16[288,1152]{1,0:T(8,128)(2,1)S(1)}, u32[]{:S(2)}, u32[]{:S(2)}) collective-permute-start(bf16[288,1152]{1,0:T(8,128)(2,1)} %copy-done.9), channel_id=1, source_target_pairs={{0,8},{2,10},{8,16},{10,18},{16,24},{18,26},{24,28},{26,30},{28,20... | collective-permute-start | bytes 1990664 | tf_op jit(solution)/shard_map/ppermute | solution.py:420
  153.6 30.8 %collective-permute-start.17 = (bf16[288,1152]{1,0:T(8,128)(2,1)}, bf16[288,1152]{1,0:T(8,128)(2,1)}, u32[]{:S(2)}, u32[]{:S(2)}) collective-permute-start(bf16[288,1152]{1,0:T(8,128)(2,1)} %collective-permute-done.14.refs_4_), channel_id=1, source_target_pairs={{0,4},{2,6},{8,0},{10,2},{16,8},{18,10},{24,16},{26,18},{28,24},{3... | collective-permute-start | bytes 1990664 | tf_op jit(solution)/shard_map/ppermute | solution.py:420
  155.8 28.6 %collective-permute-start.18 = (bf16[288,1152]{1,0:T(8,128)(2,1)}, bf16[288,1152]{1,0:T(8,128)(2,1)}, u32[]{:S(2)}, u32[]{:S(2)}) collective-permute-start(bf16[288,1152]{1,0:T(8,128)(2,1)} %copy-done.9), channel_id=1, source_target_pairs={{0,2},{2,0},{4,6},{6,4},{8,10},{10,8},{12,14},{14,12},{16,18},{18,... | collective-permute-start | bytes 1990664 | tf_op jit(solution)/shard_map/ppermute | solution.py:341
  155.8 28.6 %collective-permute-start.19 = (bf16[288,1152]{1,0:T(8,128)(2,1)}, bf16[288,1152]{1,0:T(8,128)(2,1)}, u32[]{:S(2)}, u32[]{:S(2)}) collective-permute-start(bf16[288,1152]{1,0:T(8,128)(2,1)} %collective-permute-done.14.refs_4_), channel_id=1, source_target_pairs={{0,2},{2,0},{4,6},{6,4},{8,10},{10,8},{12,14},{14,12},{16,18},{18,... | collective-permute-start | bytes 1990664 | tf_op jit(solution)/shard_map/ppermute | solution.py:341
  189.2 29.3 %collective-permute-start.20 = (bf16[288,1152]{1,0:T(8,128)(2,1)S(1)}, bf16[288,1152]{1,0:T(8,128)(2,1)S(1)}, u32[]{:S(2)}, u32[]{:S(2)}) collective-permute-start(bf16[288,1152]{1,0:T(8,128)(2,1)S(1)} %collective-permute-done.16.refs_0_), channel_id=1, source_target_pairs={{0,8},{2,10},{8,16},{10,18},{16,24},{18,26},{24,28},{26,30},{28,20... | collective-permute-start | bytes 1990664 | tf_op jit(solution)/shard_map/ppermute | solution.py:420
  189.3 36.4 %collective-permute-start.21 = (bf16[288,1152]{1,0:T(8,128)(2,1)}, bf16[288,1152]{1,0:T(8,128)(2,1)}, u32[]{:S(2)}, u32[]{:S(2)}) collective-permute-start(bf16[288,1152]{1,0:T(8,128)(2,1)} %collective-permute-done.17.refs_2_), channel_id=1, source_target_pairs={{0,4},{2,6},{8,0},{10,2},{16,8},{18,10},{24,16},{26,18},{28,24},{3... | collective-permute-start | bytes 1990664 | tf_op jit(solution)/shard_map/ppermute | solution.py:420
  191.3 34.4 %collective-permute-start.22 = (bf16[288,1152]{1,0:T(8,128)(2,1)S(1)}, bf16[288,1152]{1,0:T(8,128)(2,1)S(1)}, u32[]{:S(2)}, u32[]{:S(2)}) collective-permute-start(bf16[288,1152]{1,0:T(8,128)(2,1)S(1)} %collective-permute-done.16.refs_0_), channel_id=1, source_target_pairs={{0,2},{2,0},{4,6},{6,4},{8,10},{10,8},{12,14},{14,12},{16,18},{18,... | collective-permute-start | bytes 1990664 | tf_op jit(solution)/shard_map/ppermute | solution.py:341
  191.3 35.2 %collective-permute-start.23 = (bf16[288,1152]{1,0:T(8,128)(2,1)}, bf16[288,1152]{1,0:T(8,128)(2,1)S(1)}, u32[]{:S(2)}, u32[]{:S(2)}) collective-permute-start(bf16[288,1152]{1,0:T(8,128)(2,1)} %collective-permute-done.17.refs_2_), channel_id=1, source_target_pairs={{0,2},{2,0},{4,6},{6,4},{8,10},{10,8},{12,14},{14,12},{16,18},{18,... | collective-permute-start | bytes 1990664 | tf_op jit(solution)/shard_map/ppermute | solution.py:341
  227.4 27.6 %collective-permute-start.24 = (bf16[288,1152]{1,0:T(8,128)(2,1)S(1)}, bf16[288,1152]{1,0:T(8,128)(2,1)}, u32[]{:S(2)}, u32[]{:S(2)}) collective-permute-start(bf16[288,1152]{1,0:T(8,128)(2,1)S(1)} %collective-permute-done.20.refs_4_), channel_id=1, source_target_pairs={{0,8},{2,10},{8,16},{10,18},{16,24},{18,26},{24,28},{26,30},{28,20... | collective-permute-start | bytes 1990664 | tf_op jit(solution)/shard_map/ppermute | solution.py:420
  228.2 26.8 %collective-permute-start.25 = (bf16[288,1152]{1,0:T(8,128)(2,1)S(1)}, bf16[288,1152]{1,0:T(8,128)(2,1)}, u32[]{:S(2)}, u32[]{:S(2)}) collective-permute-start(bf16[288,1152]{1,0:T(8,128)(2,1)S(1)} %collective-permute-done.20.refs_4_), channel_id=1, source_target_pairs={{0,2},{2,0},{4,6},{6,4},{8,10},{10,8},{12,14},{14,12},{16,18},{18,... | collective-permute-start | bytes 1990664 | tf_op jit(solution)/shard_map/ppermute | solution.py:341
  228.2 26.8 %collective-permute-start.26 = (bf16[288,1152]{1,0:T(8,128)(2,1)}, bf16[288,1152]{1,0:T(8,128)(2,1)}, u32[]{:S(2)}, u32[]{:S(2)}) collective-permute-start(bf16[288,1152]{1,0:T(8,128)(2,1)} %collective-permute-done.21.refs_6_), channel_id=1, source_target_pairs={{0,2},{2,0},{4,6},{6,4},{8,10},{10,8},{12,14},{14,12},{16,18},{18,... | collective-permute-start | bytes 1990664 | tf_op jit(solution)/shard_map/ppermute | solution.py:341
  255.0 18.4 %collective-permute-start.27 = (bf16[288,1152]{1,0:T(8,128)(2,1)}, bf16[288,1152]{1,0:T(8,128)(2,1)}, u32[]{:S(2)}, u32[]{:S(2)}) collective-permute-start(bf16[288,1152]{1,0:T(8,128)(2,1)} %collective-permute-done.24.refs_8_), channel_id=1, source_target_pairs={{0,2},{2,0},{4,6},{6,4},{8,10},{10,8},{12,14},{14,12},{16,18},{18,... | collective-permute-start | bytes 1990664 | tf_op jit(solution)/shard_map/ppermute | solution.py:341
  273.5 288.8 %reduce-scatter.10.cloned.1.call-start = ((), (), s32[]{:S(2)}) async-start(), calls=%async_computation.6 | async-start | bytes 2820096
  342.0 17.6 %collective-permute-start.28 = (bf16[8,72,4608]{2,1,0:T(8,128)(2,1)}, bf16[8,72,4608]{2,1,0:T(8,128)(2,1)}, u32[]{:S(2)}, u32[]{:S(2)}) collective-permute-start(bf16[8,72,4608]{2,1,0:T(8,128)(2,1)} %dynamic-slice_bitcast_fusion), channel_id=1, source_target_pairs={{0,2},{2,0},{4,6},{6,4},{8,10},{10,8},{12,14},{14,12},{16,18},{18,... | collective-permute-start | bytes 15925256 | tf_op jit(solution)/shard_map/ppermute | solution.py:341
  368.6 29.7 %collective-permute-start.29 = (bf16[72,4608]{1,0:T(8,128)(2,1)}, bf16[72,4608]{1,0:T(8,128)(2,1)S(1)}, u32[]{:S(2)}, u32[]{:S(2)}) collective-permute-start(bf16[72,4608]{1,0:T(8,128)(2,1)} %get-tuple-element.233), channel_id=1, source_target_pairs={{0,8},{2,10},{8,16},{10,18},{16,24},{18,26},{24,28},{26,30},{28,20... | collective-permute-start | bytes 1990664 | tf_op jit(solution)/shard_map/ppermute | solution.py:498
  368.6 36.9 %collective-permute-start.30 = (bf16[72,4608]{1,0:T(8,128)(2,1)}, bf16[72,4608]{1,0:T(8,128)(2,1)S(1)}, u32[]{:S(2)}, u32[]{:S(2)}) collective-permute-start(bf16[72,4608]{1,0:T(8,128)(2,1)} %get-tuple-element.234), channel_id=1, source_target_pairs={{0,4},{2,6},{8,0},{10,2},{16,8},{18,10},{24,16},{26,18},{28,24},{3... | collective-permute-start | bytes 1990664 | tf_op jit(solution)/shard_map/ppermute | solution.py:498
  409.0 27.3 %collective-permute-start.31 = (bf16[72,4608]{1,0:T(8,128)(2,1)}, bf16[72,4608]{1,0:T(8,128)(2,1)S(1)}, u32[]{:S(2)}, u32[]{:S(2)}) collective-permute-start(bf16[72,4608]{1,0:T(8,128)(2,1)} %get-tuple-element.243), channel_id=1, source_target_pairs={{0,8},{2,10},{8,16},{10,18},{16,24},{18,26},{24,28},{26,30},{28,20... | collective-permute-start | bytes 1990664 | tf_op jit(solution)/shard_map/ppermute | solution.py:498
  409.6 26.7 %collective-permute-start.32 = (bf16[72,4608]{1,0:T(8,128)(2,1)S(1)}, bf16[72,4608]{1,0:T(8,128)(2,1)}, u32[]{:S(2)}, u32[]{:S(2)}) collective-permute-start(bf16[72,4608]{1,0:T(8,128)(2,1)S(1)} %get-tuple-element.244), channel_id=1, source_target_pairs={{0,4},{2,6},{8,0},{10,2},{16,8},{18,10},{24,16},{26,18},{28,24},{3... | collective-permute-start | bytes 1990664 | tf_op jit(solution)/shard_map/ppermute | solution.py:498
  411.0 198.8 %reduce-scatter.12.cloned.1.call-start = ((), (), s32[]{:S(2)}) async-start(), calls=%async_computation.7 | async-start | bytes 8460288
  439.6 23.6 %collective-permute-start.33 = (f32[2,4,3456]{2,1,0:T(4,128)}, f32[2,4,3456]{2,1,0:T(4,128)}, u32[]{:S(2)}, u32[]{:S(2)}) collective-permute-start(f32[2,4,3456]{2,1,0:T(4,128)} %pad_maximum_fusion.15), channel_id=1, source_target_pairs={{0,1},{1,0},{2,3},{3,2},{4,5},{5,4},{6,7},{7,6},{8,9},{9,8},{10,11... | collective-permute-start | bytes 331784 | tf_op jit(solution)/shard_map/ppermute | solution.py:341
  441.1 22.5 %collective-permute-start.34 = (bf16[72,4608]{1,0:T(8,128)(2,1)}, bf16[72,4608]{1,0:T(8,128)(2,1)}, u32[]{:S(2)}, u32[]{:S(2)}) collective-permute-start(bf16[72,4608]{1,0:T(8,128)(2,1)} %get-tuple-element.255), channel_id=1, source_target_pairs={{0,8},{2,10},{8,16},{10,18},{16,24},{18,26},{24,28},{26,30},{28,20... | collective-permute-start | bytes 1990664 | tf_op jit(solution)/shard_map/ppermute | solution.py:498
  441.7 24.0 %collective-permute-start.35 = (bf16[72,4608]{1,0:T(8,128)(2,1)S(1)}, bf16[72,4608]{1,0:T(8,128)(2,1)}, u32[]{:S(2)}, u32[]{:S(2)}) collective-permute-start(bf16[72,4608]{1,0:T(8,128)(2,1)S(1)} %get-tuple-element.256), channel_id=1, source_target_pairs={{0,4},{2,6},{8,0},{10,2},{16,8},{18,10},{24,16},{26,18},{28,24},{3... | collective-permute-start | bytes 1990664 | tf_op jit(solution)/shard_map/ppermute | solution.py:498
  443.1 22.7 %collective-permute-start.36 = (bf16[288,1152]{1,0:T(8,128)(2,1)}, bf16[288,1152]{1,0:T(8,128)(2,1)}, u32[]{:S(2)}, u32[]{:S(2)}) collective-permute-start(bf16[288,1152]{1,0:T(8,128)(2,1)} %reduce-scatter.8.cloned.1.call-done), channel_id=1, source_target_pairs={{0,1},{1,0},{2,3},{3,2},{4,5},{5,4},{6,7},{7,6},{8,9},{9,8},{10,11... | collective-permute-start | bytes 1990664 | tf_op jit(solution)/shard_map/ppermute | solution.py:341
  471.4 21.1 %collective-permute-start.37 = (bf16[72,4608]{1,0:T(8,128)(2,1)}, bf16[72,4608]{1,0:T(8,128)(2,1)}, u32[]{:S(2)}, u32[]{:S(2)}) collective-permute-start(bf16[72,4608]{1,0:T(8,128)(2,1)} %fusion.96), channel_id=1, source_target_pairs={{0,8},{2,10},{8,16},{10,18},{16,24},{18,26},{24,28},{26,30},{28,20... | collective-permute-start | bytes 1990664 | tf_op jit(solution)/shard_map/ppermute | solution.py:498
  477.8 14.6 %collective-permute-start.38 = (bf16[8,3456]{1,0:T(8,128)(2,1)}, bf16[8,3456]{1,0:T(8,128)(2,1)S(1)}, u32[]{:S(2)}, u32[]{:S(2)}) collective-permute-start(bf16[8,3456]{1,0:T(8,128)(2,1)} %reshape.495), channel_id=1, source_target_pairs={{0,16},{2,18},{4,20},{6,22},{8,24},{10,26},{12,28},{14,30},{16,0},... | collective-permute-start | bytes 165896 | tf_op jit(solution)/shard_map/ppermute | solution.py:341
  494.9 19.6 %collective-permute-start.39 = (bf16[72,4608]{1,0:T(8,128)(2,1)S(1)}, bf16[72,4608]{1,0:T(8,128)(2,1)}, u32[]{:S(2)}, u32[]{:S(2)}) collective-permute-start(bf16[72,4608]{1,0:T(8,128)(2,1)S(1)} %fusion.98), channel_id=1, source_target_pairs={{0,1},{1,0},{2,3},{3,2},{4,5},{5,4},{6,7},{7,6},{8,9},{9,8},{10,11... | collective-permute-start | bytes 1990664 | tf_op jit(solution)/shard_map/ppermute | solution.py:341
  496.6 17.8 %collective-permute-start.40 = (bf16[2,8,3456]{2,1,0:T(8,128)(2,1)}, bf16[2,8,3456]{2,1,0:T(8,128)(2,1)}, u32[]{:S(2)}, u32[]{:S(2)}) collective-permute-start(bf16[2,8,3456]{2,1,0:T(8,128)(2,1)} %pad_maximum_fusion.16), channel_id=1, source_target_pairs={{0,8},{2,10},{4,12},{6,14},{8,0},{10,2},{12,4},{14,6},{16,24},{18,... | collective-permute-start | bytes 331784 | tf_op jit(solution)/shard_map/ppermute | solution.py:341
  515.5 18.6 %collective-permute-start.41 = (bf16[2,2,8,3456]{3,2,1,0:T(8,128)(2,1)S(1)}, bf16[2,2,8,3456]{3,2,1,0:T(8,128)(2,1)S(1)}, u32[]{:S(2)}, u32[]{:S(2)}) collective-permute-start(bf16[2,2,8,3456]{3,2,1,0:T(8,128)(2,1)S(1)} %pad_maximum_fusion.11), channel_id=1, source_target_pairs={{0,4},{2,6},{4,0},{6,2},{8,12},{10,14},{12,8},{14,10},{16,20},{18,... | collective-permute-start | bytes 663560 | tf_op jit(solution)/shard_map/ppermute | solution.py:341
  518.5 15.6 %collective-permute-start.42 = (bf16[1,4,4,16,1152]{4,3,2,1,0:T(8,128)(2,1)}, bf16[1,4,4,16,1152]{4,3,2,1,0:T(8,128)(2,1)S(1)}, u32[]{:S(2)}, u32[]{:S(2)}) collective-permute-start(bf16[1,4,4,16,1152]{4,3,2,1,0:T(8,128)(2,1)} %slice.353), channel_id=1, source_target_pairs={{0,1},{1,0},{2,3},{3,2},{4,5},{5,4},{6,7},{7,6},{8,9},{9,8},{10,11... | collective-permute-start | bytes 1769480 | tf_op jit(solution)/shard_map/ppermute | solution.py:609
  534.2 10.1 %collective-permute-start.43 = (bf16[2,2,2,8,3456]{4,3,2,1,0:T(8,128)(2,1)S(1)}, bf16[2,2,2,8,3456]{4,3,2,1,0:T(8,128)(2,1)S(1)}, u32[]{:S(2)}, u32[]{:S(2)}) collective-permute-start(bf16[2,2,2,8,3456]{4,3,2,1,0:T(8,128)(2,1)S(1)} %pad_maximum_fusion.7), channel_id=1, source_target_pairs={{0,2},{2,0},{4,6},{6,4},{8,10},{10,8},{12,14},{14,12},{16,18},{18,... | collective-permute-start | bytes 1327112 | tf_op jit(solution)/shard_map/ppermute | solution.py:341
  534.3 15.7 %collective-permute-start.44 = (bf16[1,4,4,16,1152]{4,3,2,1,0:T(8,128)(2,1)S(1)}, bf16[1,4,4,16,1152]{4,3,2,1,0:T(8,128)(2,1)S(1)}, u32[]{:S(2)}, u32[]{:S(2)}) collective-permute-start(bf16[1,4,4,16,1152]{4,3,2,1,0:T(8,128)(2,1)S(1)} %slice.352), channel_id=1, source_target_pairs={{0,1},{1,0},{2,3},{3,2},{4,5},{5,4},{6,7},{7,6},{8,9},{9,8},{10,11... | collective-permute-start | bytes 1769480 | tf_op jit(solution)/shard_map/ppermute | solution.py:609
  551.3 6.1 collective-permute-start.45
  557.5 4.4 collective-permute-start.46
  562.2 13.9 %collective-permute-start.47 = (bf16[2,2,72,128]{3,2,0,1:T(8,128)(2,1)S(1)}, bf16[2,2,72,128]{3,2,0,1:T(8,128)(2,1)S(1)}, u32[]{:S(2)}, u32[]{:S(2)}) collective-permute-start(bf16[2,2,72,128]{3,2,0,1:T(8,128)(2,1)S(1)} %pad_maximum_fusion.17), channel_id=1, source_target_pairs={{0,4},{2,6},{4,0},{6,2},{8,12},{10,14},{12,8},{14,10},{16,20},{18,... | collective-permute-start | bytes 221192 | tf_op jit(solution)/shard_map/ppermute | solution.py:341
  563.0 13.1 %collective-permute-start.48 = (f32[12,1152]{1,0:T(8,128)S(1)}, f32[12,1152]{1,0:T(8,128)S(1)}, u32[]{:S(2)}, u32[]{:S(2)}) collective-permute-start(f32[12,1152]{1,0:T(8,128)S(1)} %concatenate.34), channel_id=1, source_target_pairs={{0,2},{2,0},{4,6},{6,4},{8,10},{10,8},{12,14},{14,12},{16,18},{18,... | collective-permute-start | bytes 165896 | tf_op jit(solution)/shard_map/ppermute | solution.py:341
  563.0 13.1 %collective-permute-start.49 = (bf16[72,1152]{1,0:T(8,128)(2,1)}, bf16[72,1152]{1,0:T(8,128)(2,1)S(1)}, u32[]{:S(2)}, u32[]{:S(2)}) collective-permute-start(bf16[72,1152]{1,0:T(8,128)(2,1)} %reduce-scatter.10.cloned.1.call-done), channel_id=1, source_target_pairs={{0,1},{1,0},{2,3},{3,2},{4,5},{5,4},{6,7},{7,6},{8,9},{9,8},{10,11... | collective-permute-start | bytes 497672 | tf_op jit(solution)/shard_map/ppermute | solution.py:341
  576.2 6.8 %collective-permute-start.50 = (bf16[2,2,2,72,128]{4,3,0,1,2:T(8,128)(2,1)S(1)}, bf16[2,2,2,72,128]{4,3,0,1,2:T(8,128)(2,1)S(1)}, u32[]{:S(2)}, u32[]{:S(2)}) collective-permute-start(bf16[2,2,2,72,128]{4,3,0,1,2:T(8,128)(2,1)S(1)} %pad_maximum_fusion.12), channel_id=1, source_target_pairs={{0,2},{2,0},{4,6},{6,4},{8,10},{10,8},{12,14},{14,12},{16,18},{18,... | collective-permute-start | bytes 442376 | tf_op jit(solution)/shard_map/ppermute | solution.py:341
  576.5 6.5 %collective-permute-start.51 = (f32[12,1152]{1,0:T(8,128)S(1)}, f32[12,1152]{1,0:T(8,128)S(1)}, u32[]{:S(2)}, u32[]{:S(2)}) collective-permute-start(f32[12,1152]{1,0:T(8,128)S(1)} %add.584), channel_id=1, source_target_pairs={{0,4},{2,6},{4,0},{6,2},{8,12},{10,14},{12,8},{14,10},{16,20},{18,... | collective-permute-start | bytes 165896 | tf_op jit(solution)/shard_map/ppermute | solution.py:341
  583.3 5.4 collective-permute-start.52
  584.9 9.3 %collective-permute-start.53 = (f32[12,1152]{1,0:T(8,128)S(1)}, f32[12,1152]{1,0:T(8,128)S(1)}, u32[]{:S(2)}, u32[]{:S(2)}) collective-permute-start(f32[12,1152]{1,0:T(8,128)S(1)} %add.585), channel_id=1, source_target_pairs={{0,8},{2,10},{4,12},{6,14},{8,0},{10,2},{12,4},{14,6},{16,24},{18,... | collective-permute-start | bytes 165896 | tf_op jit(solution)/shard_map/ppermute | solution.py:341
  594.2 4.0 collective-permute-start.54
  594.3 5.7 collective-permute-start.55
  600.0 5.5 collective-permute-start.56
  601.1 4.4 collective-permute-start.57
  605.5 4.3 collective-permute-start.58
  609.8 14.2 %collective-permute-start.59 = (bf16[72,3456]{1,0:T(8,128)(2,1)}, bf16[72,3456]{1,0:T(8,128)(2,1)S(1)}, u32[]{:S(2)}, u32[]{:S(2)}) collective-permute-start(bf16[72,3456]{1,0:T(8,128)(2,1)} %reduce-scatter.12.cloned.1.call-done), channel_id=1, source_target_pairs={{0,1},{1,0},{2,3},{3,2},{4,5},{5,4},{6,7},{7,6},{8,9},{9,8},{10,11... | collective-permute-start | bytes 1493000 | tf_op jit(solution)/shard_map/ppermute | solution.py:341
  (75 other events, 811.4 us)
Sparse Core Ops, SparseCore 0:
  10.9 101.4 all-gather.2
  114.7 109.1 all-gather.4
  273.6 132.9 reduce-scatter.7
  411.2 74.6 reduce-scatter.9
  490.4 107.7 reduce-scatter.11
where the time goes:
time: 642 us; the launch traced here: 633 us
  matrix products  202 us (31%)
  waiting for transfers between devices  142 us (22%)
  Pallas kernels  96.4 us (15%)
  other arithmetic  64.6 us (10%)
  starting transfers between devices  62.5 us (10%)
  local copies, waits for them, and re-layouts  49.1 us (8%)
  between operations  15.9 us (2%)
    ppermute x43, waiting for transfers between devices, trade(): return lax.ppermute(block, axis, [(i, i ^ bit) for i in range(size)])  84.2 us
    dot_general x7, matrix products, low_dot(): return jnp.dot(left, right, preferred_element_type=jnp.float32)  75.2 us
    ppermute x14, waiting for transfers between devices, fly(): lax.ppermute(block, 'seq', ring_path(self.chips, step))  49.2 us
    pallas_call x2, Pallas kernels, attend_back(): pl.pallas_call(functools.partial(attend_back_kernel, own=own, total=total...  45.3 us
    ppermute x43, starting transfers between devices, trade(): return lax.ppermute(block, axis, [(i, i ^ bit) for i in range(size)])  43.8 us
    pallas_call x1, Pallas kernels, attend(): pl.pallas_call(functools.partial(attend_kernel, own=own, total=total), gr...  27.9 us
    unnamed x148, local copies, waits for them, and re-layouts  26.7 us
    dot_general x2, matrix products, back_mixed(): jnp.einsum('spcge,de->spcgd', rows, full_mix, preferred_element_type=jnp....  22.4 us
  transfers between devices with their start and end apart: 65, of which 29 were waited for; matrix products, arithmetic and copies ran while one was open for 45% of the time, Pallas kernels for 15%

commit v1 on v0

--- a/solution.py
+++ b/solution.py
@@ -353,7 +353,7 @@
     return block.reshape((size,) + block.shape[axis:])
 
 
-def scatter_small(block):
+def scatter_small(block, sent_as=jnp.float32):
     size = lax.axis_size("seq")
     place = lax.axis_index("seq")
     bit = 1
@@ -362,7 +362,7 @@
         upper = (place & bit) > 0
         kept = jnp.where(upper, block[:, 1], block[:, 0])
         sent = jnp.where(upper, block[:, 0], block[:, 1])
-        block = kept + trade(sent, "seq", bit)
+        block = kept + trade(sent.astype(sent_as), "seq", bit).astype(jnp.float32)
         bit *= 2
     return block[0]
 
@@ -540,12 +540,15 @@
 class AllSum:
     def __init__(self, block):
         self.block = block
-        self.rounds = []
-        for axis in ("seq", "rows"):
-            bit = 1
-            while bit < lax.axis_size(axis):
-                self.rounds.append((axis, bit))
-                bit *= 2
+        self.rounds = [("seq", [1])]
+        bit, rows = 2, 1
+        while bit < lax.axis_size("seq"):
+            pair = bit * 2 < lax.axis_size("seq")
+            self.rounds.append(("seq", [bit, 2 * bit, 3 * bit] if pair else [bit]))
+            bit *= 4 if pair else 2
+        while rows < lax.axis_size("rows"):
+            self.rounds.append(("rows", [rows]))
+            rows *= 2
 
     def pending(self):
         return bool(self.rounds)
@@ -554,10 +557,13 @@
         return (self.block,)
 
     def fly(self, loads):
-        return (trade(loads[0], *self.rounds[0]),)
+        axis, partners = self.rounds[0]
+        return tuple(trade(loads[0], axis, partner) for partner in partners)
 
     def land(self, loads, gots):
         self.block = loads[0] + gots[0]
+        if len(gots) == 3:
+            self.block = self.block + (gots[1] + gots[2])
         self.rounds.pop(0)
 
 
@@ -576,14 +582,26 @@
     def load(self):
         return (self.block,)
 
+    def partners(self):
+        return [self.bit // 2, self.bit, self.bit + self.bit // 2] if self.bit > 2 else [self.bit]
+
     def fly(self, loads):
-        return (trade(loads[0], "seq", self.bit),)
+        return tuple(trade(loads[0], "seq", partner) for partner in self.partners())
 
     def land(self, loads, gots):
-        upper = (lax.axis_index("seq") & self.bit) > 0
-        ends = [jnp.where(upper, gots[0], loads[0]), jnp.where(upper, loads[0], gots[0])]
-        self.block = jnp.stack(ends, axis=self.axis)
-        self.axis, self.bit = self.axis + 1, self.bit // 2
+        bits = [self.bit, self.bit // 2] if len(gots) == 3 else [self.bit]
+        place = lax.axis_index("seq")
+        blocks = list(loads + gots)
+        for flip, bit in enumerate(bits[::-1]):
+            upper = (place & bit) > 0
+            blocks = [
+                jnp.where(upper, blocks[i ^ (1 << flip)], blocks[i]) for i in range(len(blocks))
+            ]
+        if len(bits) == 2:
+            blocks = [jnp.stack(blocks[:2], axis=self.axis), jnp.stack(blocks[2:], axis=self.axis)]
+        self.block = jnp.stack(blocks, axis=self.axis)
+        self.axis += len(bits)
+        self.bit = bits[-1] // 2
         if self.bit == 0:
             shape = self.block.shape[self.axis :]
             following = self.follow(self.block.reshape((-1,) + shape[1:]))
@@ -697,8 +715,7 @@
     def my_part(array, part, axis):
         return lax.dynamic_slice_in_dim(array, place * part, part, axis=axis)
 
-    full_first = lax.all_gather(jnp.concatenate([mix_weight, proj_weight], axis=1), "seq", axis=0, tiled=True)
-    full_mix, full_proj = full_first[:, : 3 * D], full_first[:, 3 * D :]
+    full_mix = lax.all_gather(mix_weight, "seq", axis=0, tiled=True)
     borrowed, borrowed_at, sent_rows = borrow_rows(act_tokens, row_shards)
     timestep, time_in_weight = lax.optimization_barrier((timestep, time_in_weight, sent_rows))[:2]
     half_width = FREQ // 2
@@ -726,16 +743,17 @@
 
     def time_third(time_embed):
         partial = jnp.einsum("di,de->ie", time_embed, time_mix_weight, preferred_element_type=jnp.float32)
-        return (scatter_small(partial.reshape(seqs, seq_rows * PACK, 3 * D)),)
-
-    features, time_pre = time_first(timestep, time_in_weight)
-    time_hidden, time_embed = time_second(time_pre)
+        return (scatter_small(partial.reshape(seqs, seq_rows * PACK, 3 * D), jnp.bfloat16),)
+
+    proj_ring = RingGather(proj_weight)
+    features, time_pre = slot([proj_ring], time_first, timestep, time_in_weight)
+    time_hidden, time_embed = slot([proj_ring], time_second, time_pre)
     key_at = jnp.concatenate([jnp.arange(local_rows), borrowed_at])
     key_row = lax.axis_index("rows") * local_rows + key_at
     key_rows = jnp.where((key_row >= 0) & (key_row < GRID), key_at, 4 * GRID).astype(jnp.int32)
     table = bias_table(position_bias, key_rows, local_rows)
     time_embed = after(time_embed, table)
-    (time_proj,) = time_third(time_embed)
+    (time_proj,) = slot([proj_ring], time_third, time_embed)
     time_proj = time_proj.reshape(seq_rows, PACK, 3 * D)
     my_features = my_part(features, freq_part, 1)
     block_slots = image_ids[:, ::GRID]
@@ -747,15 +765,19 @@
     ext_rows = ext_tokens.shape[1]
     ext_count = seq_rows * ext_rows * columns
 
-    normed1 = norm_forward(ext_tokens.astype(jnp.float32), norm1_gain, norm1_shift)[0].astype(jnp.bfloat16)
+    normed1, _, inverse_one = norm_forward(ext_tokens.astype(jnp.float32), norm1_gain, norm1_shift)
+    normed1 = normed1.astype(jnp.bfloat16)
+    mean_one = jnp.mean(act_tokens.astype(jnp.float32), axis=-1, keepdims=True)
+    inverse_one = inverse_one[:, :local_rows]
     full_up = lax.all_gather(up_weight, "seq", axis=0, tiled=True)
-    down_ring = RingGather(after(down_weight, full_first[:8, :128]))
+    down_ring = RingGather(after(down_weight, full_mix[:8, :128]))
 
     def to_mixed(normed1):
         return ((low_dot(normed1, full_mix) + unit_time[:, None, :, None, :]).astype(jnp.bfloat16),)
 
-    (mixed,) = slot([down_ring], to_mixed, normed1)
-    (attended,) = slot([down_ring], lambda mixed: (attend(mixed, table, local_rows),), mixed)
+    (mixed,) = slot([proj_ring], to_mixed, normed1)
+    (attended,) = slot([down_ring, proj_ring], lambda mixed: (attend(mixed, table, local_rows),), mixed)
+    full_proj = proj_ring.whole()
     flat_tokens = act_tokens.astype(jnp.float32)
 
     def second_norm(attended):
@@ -780,14 +802,17 @@
     flat_hidden = hidden.reshape(token_count, FF)
     flat_cot = act_cot.reshape(token_count, D)
 
+    raw = {}
+
     def weight_down(flat_hidden):
         grad = jnp.einsum("nf,nd->fd", flat_hidden, flat_cot, preferred_element_type=jnp.float32)
-        return (grad.astype(jnp.bfloat16),)
+        raw["down"] = grad.astype(jnp.bfloat16)
+        return (raw["down"],)
 
     (grad_down_w,) = slot([down_ring], weight_down, flat_hidden)
     full_down = down_ring.whole()
     grad_down_b = jnp.sum(flat_cot, axis=0, dtype=jnp.float32)
-    down_part = lax.psum_scatter(grad_down_w, "seq", scatter_dimension=0, tiled=True)
+    down_part = lax.psum_scatter(raw["down"], "seq", scatter_dimension=0, tiled=True)
     grad_hidden = jnp.einsum(
         "nd,fd->nf", flat_cot, full_down, preferred_element_type=jnp.float32
     )
@@ -808,6 +833,7 @@
         grad_proj_w = jnp.einsum(
             "nd,ne->de", attended.reshape(token_count, D), grad_branch, preferred_element_type=jnp.float32
         ).astype(jnp.bfloat16)
+        raw["proj"] = grad_proj_w
         grad_proj_b = jnp.sum(grad_branch, axis=0, dtype=jnp.float32)
         grad_attended = jnp.einsum(
             "ne,de->nd", grad_branch, full_proj, preferred_element_type=jnp.float32
@@ -821,7 +847,7 @@
     (grad_residual, grad_gain_two, grad_shift_two, grad_proj_w, grad_proj_b, grad_attended) = slot(
         [up_sum], back_norm, grad_normed2
     )
-    proj_part = lax.psum_scatter(grad_proj_w, "seq", scatter_dimension=0, tiled=True)
+    proj_part = lax.psum_scatter(raw["proj"], "seq", scatter_dimension=0, tiled=True)
     part = -(-seq_rows // 2)
     spans = [slice(0, part), slice(part, seq_rows)][: min(2, seq_rows)]
     grad_mixed, grad_tables, grad_units = None, [], []
@@ -842,7 +868,8 @@
             grad_mixed.reshape(ext_count, 3 * D),
             preferred_element_type=jnp.float32,
         )
-        return (grad_mix_w.astype(jnp.bfloat16),)
+        raw["mix"] = grad_mix_w.astype(jnp.bfloat16)
+        return (raw["mix"],)
 
     (grad_mix_w,) = slot([unit_sum, up_sum, down_sum], weight_mix, grad_mixed)
     found = {}
@@ -866,7 +893,7 @@
 
     grad_time_proj = jnp.einsum("skp,ske->spe", slot_hot, unit_sum.total, precision=highest)
     chain = Chain(grad_time_proj.astype(jnp.bfloat16).reshape(-1, 3 * D), from_time_proj)
-    mix_part = lax.psum_scatter(grad_mix_w, "seq", scatter_dimension=0, tiled=True)
+    mix_part = lax.psum_scatter(raw["mix"], "seq", scatter_dimension=0, tiled=True)
     first_sums = (grad_proj_b, grad_gain_two, grad_shift_two, grad_up_b, grad_down_b)
     rings = [up_sum, chain]
 
@@ -879,8 +906,8 @@
         return (grad_in[:, :local_rows], grad_in[:, local_rows:].astype(jnp.bfloat16))
 
     def back_first(grad_normed1, tokens, grad_residual, span):
-        _, unit_one, inverse_one = norm_forward(tokens[span].astype(jnp.float32), norm1_gain, norm1_shift)
-        grad_norm_one, gain, shift = norm_backward(grad_normed1, unit_one, inverse_one, norm1_gain)
+        unit_one = (tokens[span].astype(jnp.float32) - mean_one[span]) * inverse_one[span]
+        grad_norm_one, gain, shift = norm_backward(grad_normed1, unit_one, inverse_one[span], norm1_gain)
         return ((grad_residual[span] + grad_norm_one).astype(jnp.bfloat16), gain, shift)
 
     def last_part(hidden, residual, span):
@@ -903,15 +930,18 @@
     grad_gain_one, grad_shift_one = (sum(part) for part in zip(*[first[1:] for first in firsts]))
     late_sums = (grad_gain_one, grad_shift_one, bias_grad) + first_sums
     late_sum = AllSum(in_rows(late_sums))
-    proj_sum, mix_sum = RowSum(proj_part), RowSum(mix_part)
+    proj_sum = RowSum(proj_part)
     rings += [late_sum, proj_sum]
     for span in spans[1:]:
         finish(span)
     output = jnp.concatenate(outputs, axis=0)
     tokens_grad = jnp.concatenate(tokens_grads, axis=0)
+    run(lambda: ())
+    mix_sum = RowSum(after(mix_part, chain.block))
+    mix_got = mix_sum.fly(mix_sum.load())
     while any(ring.pending() for ring in rings):
         run(lambda: ())
-    slot([mix_sum], lambda: ())
+    mix_sum.land(mix_sum.load(), mix_got)
 
     (gain_one, shift_one, bias_total, proj_total, gain_two, shift_two, up_total, down_total) = from_rows(
         late_sum.block, late_sums

time: 642 us -> 632 us (0.984)
  waiting for transfers between devices: 142 us -> 118 us
  starting transfers between devices: 62.5 us -> 72 us
  Pallas kernels: 96.4 us -> 103 us
    ppermute x14 -> x21, waiting for transfers between devices: 49.2 us -> 35 us  [fly(): lax.ppermute(block, 'seq', ring_path(self.chips, step))]
    ppermute x14 -> x21, starting transfers between devices: 15 us -> 22.8 us  [fly(): lax.ppermute(block, 'seq', ring_path(self.chips, step))]
    pallas_call x2 -> x3, Pallas kernels: 11.1 us -> 17.8 us  [assemble(): pl.pallas_call(functools.partial(assemble_kernel, count=len(pieces)), gri...]
    unnamed x148 -> x178, local copies, waits for them, and re-layouts: 26.7 us -> 20.6 us
    ppermute x43 -> x55, waiting for transfers between devices: 84.2 us -> 79.7 us  [trade(): return lax.ppermute(block, axis, [(i, i ^ bit) for i in range(size)])]
    ppermute x43 -> x55, starting transfers between devices: 43.8 us -> 44.9 us  [trade(): return lax.ppermute(block, axis, [(i, i ^ bit) for i in range(size)])]
  transfers between devices with their start and end apart: 65 -> 84, of which waited for: 29 -> 31; matrix products, arithmetic and copies ran while one was open for 45% -> 47% of each run, Pallas kernels for 15% -> 17%
where the time goes in v1:
time: 632 us; the launch traced here: 624 us
  matrix products  201 us (32%)
  waiting for transfers between devices  118 us (19%)
  Pallas kernels  103 us (16%)
  starting transfers between devices  72 us (11%)
  other arithmetic  64.5 us (10%)
  local copies, waits for them, and re-layouts  49.9 us (8%)
  between operations  16.2 us (3%)
    ppermute x55, waiting for transfers between devices, trade(): return lax.ppermute(block, axis, [(i, i ^ bit) for i in range(size)])  79.7 us
    dot_general x7, matrix products, low_dot(): return jnp.dot(left, right, preferred_element_type=jnp.float32)  73.7 us
    pallas_call x2, Pallas kernels, attend_back(): pl.pallas_call(functools.partial(attend_back_kernel, own=own, total=total...  45.1 us
    ppermute x55, starting transfers between devices, trade(): return lax.ppermute(block, axis, [(i, i ^ bit) for i in range(size)])  44.9 us
    ppermute x21, waiting for transfers between devices, fly(): lax.ppermute(block, 'seq', ring_path(self.chips, step))  35 us
    pallas_call x1, Pallas kernels, attend(): pl.pallas_call(functools.partial(attend_kernel, own=own, total=total), gr...  27.8 us
    dot_general x2, matrix products, back_mixed(): jnp.einsum('spcge,de->spcgd', rows, full_mix, preferred_element_type=jnp....  23 us
    ppermute x21, starting transfers between devices, fly(): lax.ppermute(block, 'seq', ring_path(self.chips, step))  22.8 us
  transfers between devices with their start and end apart: 84, of which 31 were waited for; matrix products, arithmetic and copies ran while one was open for 47% of the time, Pallas kernels for 17%

profile of v1, /device:TPU:0, one launch (start us, length us, event | category | flops | bytes accessed | tf_op | source)
XLA Modules:
  0.0 624.0 jit_solution(4348486939435226511)
XLA Ops:
  8.0 2.4 constant_dynamic-slice_fusion
  12.1 4.1 collective-permute-start.1
  16.2 2.7 collective-permute-done.1
  20.4 4.1 collective-permute-done.2
  25.8 8.0 %collective-permute-done.3 = bf16[2,2,18,1152]{3,2,0,1:T(8,128)(2,1)S(1)} collective-permute-done((bf16[2,2,18,1152]{3,2,0,1:T(8,128)(2,1)S(1)}, bf16[2,2,18,1152]{3,2,0,1:T(8,128)(2,1)S(1)}, u32[]{:S(2)}, u32[]{:S(2)}) %collective-permute-start.3) | collective-permute-done | bytes 165920 | tf_op jit(solution)/shard_map/ppermute | solution.py:341
  38.7 4.7 collective-permute-done.5.refs_2_
  51.3 7.9 %collective-permute-done.9 = f32[4,72,128]{2,1,0:T(8,128)S(1)} collective-permute-done((f32[4,72,128]{2,1,0:T(8,128)}, f32[4,72,128]{2,1,0:T(8,128)S(1)}, u32[]{:S(2)}, u32[]{:S(2)}) %collective-permute-start.9) | collective-permute-done | bytes 147488 | tf_op jit(solution)/shard_map/ppermute | solution.py:341
  61.0 7.6 %collective-permute-done.10 = f32[2,72,128]{2,1,0:T(8,128)S(1)} collective-permute-done((f32[2,72,128]{2,1,0:T(8,128)S(1)}, f32[2,72,128]{2,1,0:T(8,128)S(1)}, u32[]{:S(2)}, u32[]{:S(2)}) %collective-permute-start.10) | collective-permute-done | bytes 73760 | tf_op jit(solution)/shard_map/ppermute | solution.py:341
  74.3 6.9 %bias_table.1.table_ref = f32[16,192,128]{2,1,0:T(8,128)} custom-call(f32[16,81]{1,0:T(8,128)} %reshape.552.bias_ref, s32[12]{0:T(128)} %and_select_fusion.row_ref.refs_2_), custom_call_target="tpu_custom_call" | custom-call | tf_op jit(solution)/shard_map/bias_table/pallas_call | solution.py:125
  81.2 2.6 collective-permute-start.12
  85.2 5.6 collective-permute-done.12.refs_6_
  90.7 2.0 collective-permute-done.13.refs_8_
  99.3 1.8 convert_reduce_fusion.1
  103.1 2.4 fusion.13
  105.4 8.3 %collective-permute-done.17 = bf16[4,8,3456]{2,1,0:T(8,128)(2,1)S(1)} collective-permute-done((bf16[4,8,3456]{2,1,0:T(8,128)(2,1)S(1)}, bf16[4,8,3456]{2,1,0:T(8,128)(2,1)S(1)}, u32[]{:S(2)}, u32[]{:S(2)}) %collective-permute-start.17) | collective-permute-done | bytes 221216 | tf_op jit(solution)/shard_map/ppermute | solution.py:341
  115.6 9.1 %collective-permute-done.18 = bf16[2,8,3456]{2,1,0:T(8,128)(2,1)S(1)} collective-permute-done((bf16[2,8,3456]{2,1,0:T(8,128)(2,1)S(1)}, bf16[2,8,3456]{2,1,0:T(8,128)(2,1)S(1)}, u32[]{:S(2)}, u32[]{:S(2)}) %collective-permute-start.18) | collective-permute-done | bytes 110624 | tf_op jit(solution)/shard_map/ppermute | solution.py:341
  124.8 3.7 fusion.16
  128.6 4.6 collective-permute-done.19
  134.8 20.2 %add_convert_fusion.mixed_ref = bf16[2,12,4,16,3456]{4,3,2,1,0:T(8,128)(2,1)} fusion(bf16[2,12,4,16,1152]{4,3,2,1,0:T(8,128)(2,1)} %fusion.16, f32[2,4,3456]{2,1,0:T(4,128)S(1)} %fusion.96, bf16[1152,3456]{1,0:T(8,128)(2,1)} %all-gather.3.cloned.1.call-done), kind=kOutput, calls=%fused_computation | convolution fusion | flops 12241207296 | bytes 22228992 | tf_op jit(solution)/shard_map/dot_general | solution.py:29
  155.0 2.0 collective-permute-start.28
  157.7 27.8 %attend.1 = bf16[2,8,4,16,1152]{4,3,2,1,0:T(8,128)(2,1)S(1)} custom-call(bf16[2,12,4,16,3456]{4,3,2,1,0:T(8,128)(2,1)} %add_convert_fusion.mixed_ref, f32[16,192,128]{2,1,0:T(8,128)S(1)} %copy-done.1), custom_call_target="tpu_custom_call" | custom-call | tf_op jit(solution)/shard_map/attend/pallas_call | solution.py:285
  185.7 11.8 %collective-permute-done.28.refs_2_ = bf16[288,1152]{1,0:T(8,128)(2,1)S(1)} collective-permute-done((bf16[288,1152]{1,0:T(8,128)(2,1)}, bf16[288,1152]{1,0:T(8,128)(2,1)S(1)}, u32[]{:S(2)}, u32[]{:S(2)}) %collective-permute-start.28) | collective-permute-done | bytes 663584 | tf_op jit(solution)/shard_map/ppermute | solution.py:420
  197.5 2.7 assemble.3.refs_14_
  203.0 6.5 %assemble.4 = bf16[16,72,1152]{2,1,0:T(8,128)(2,1)S(1)} custom-call(s32[16]{0:T(128)S(1)} %stack.273.at_ref, bf16[72,1152]{1,0:T(8,128)(2,1)S(1)} %copy-done.15, bf16[72,1152]{1,0:T(8,128)(2,1)S(1)} %copy-done.21, bf16[72,1152]{1,0:T(8,128)(2,1)S(1)} %copy-done.17, bf16[72,1152]{1,0:T(8,128)(2,1)S(1)} %copy-done.27, bf16[72,1152]{1,0:T(8,128)(2,1)S(1)} %copy-done.19, ...), custom_call_target="tpu_custom_call" | custom-call | tf_op jit(solution)/shard_map/assemble/pallas_call | solution.py:151
  209.5 3.8 fusion.105
  215.1 3.8 add_convert_fusion.2
  223.3 26.3 %add_convert_fusion.1 = (bf16[2,8,4,16,4608]{4,3,2,1,0:T(8,128)(2,1)}, bf16[2,8,4,16,4608]{4,3,2,1,0:T(8,128)(2,1)S(1)}) fusion(f32[4608]{0:T(1024)S(1)} %copy-done.74, bf16[2,8,4,16,1152]{4,3,2,1,0:T(8,128)(2,1)} %get-tuple-element.272, bf16[1152,4608]{1,0:T(8,128)(2,1)} %all-gather.5.cloned.1.call-done), kind=kOutput, calls=%fused_computation.6 | convolution fusion | flops 10966007808 | bytes 31868928 | tf_op jit(solution)/shard_map/dot_general | solution.py:29
  253.2 14.8 %convolution_convert_fusion.1 = bf16[4608,1152]{1,0:T(8,128)(2,1)} fusion(bf16[1024,4608]{1,0:T(8,128)(2,1)S(1)} %bitcast.512, bf16[1024,1152]{1,0:T(8,128)(2,1)S(1)} %bitcast.486), kind=kOutput, calls=%fused_computation.2 | convolution fusion | flops 10876944384 | bytes 22413312 | tf_op jit(solution)/shard_map/nf,nd->fd/dot_general | solution.py:808
  268.6 2.0 collective-permute-done.42.refs_13_
  272.8 8.6 %assemble.5 = bf16[16,288,1152]{2,1,0:T(8,128)(2,1)} custom-call(s32[14]{0:T(128)S(1)} %stack.274.at_ref, bf16[288,1152]{1,0:T(8,128)(2,1)S(1)} %collective-permute-done.27.refs_0_, bf16[288,1152]{1,0:T(8,128)(2,1)S(1)} %copy-done.11, bf16[288,1152]{1,0:T(8,128)(2,1)S(1)} %collective-permute-done.28.refs_2_, ...), custom_call_target="tpu_custom_call", output_to_operand_aliasing={{}: (15, {})} | custom-call | tf_op jit(solution)/shard_map/assemble/pallas_call | solution.py:151
  281.4 21.5 %convert_reduce_fusion = (f32[4608]{0:T(1024)S(1)}, bf16[1024,4608]{1,0:T(8,128)(2,1)}) fusion(bf16[2,8,4,16,4608]{4,3,2,1,0:T(8,128)(2,1)} %get-tuple-element.293, bf16[4608,1152]{1,0:T(8,128)(2,1)} %bitcast.473, bf16[1024,1152]{1,0:T(8,128)(2,1)S(1)} %bitcast.487), kind=kOutput, calls=%fused_computation.5 | convolution fusion | flops 10895224832 | bytes 31868928 | tf_op jit(solution)/shard_map/nd,fd->nf/dot_general | solution.py:816
  302.9 17.2 %convolution_convert_fusion = bf16[1152,4608]{1,0:T(8,128)(2,1)} fusion(bf16[1024,1152]{1,0:T(8,128)(2,1)S(1)} %bitcast.501, bf16[1024,4608]{1,0:T(8,128)(2,1)} %get-tuple-element.502), kind=kOutput, calls=%fused_computation.1 | convolution fusion | flops 10876944384 | bytes 22413312 | tf_op jit(solution)/shard_map/nd,nf->df/dot_general | solution.py:821
  320.1 5.3 dynamic-slice_bitcast_fusion
  325.4 16.1 %fusion.107 = f32[1024,1152]{1,0:T(8,128)S(1)} fusion(bf16[1024,4608]{1,0:T(8,128)(2,1)} %get-tuple-element.502, bf16[1152,4608]{1,0:T(8,128)(2,1)} %all-gather.5.cloned.1.call-done), kind=kOutput, calls=%fused_computation.262 | convolution fusion | flops 10871635968 | bytes 24772608 | tf_op jit(solution)/shard_map/nf,df->nd/dot_general | solution.py:824
  343.8 3.2 convert_reduce_fusion.3
  347.0 5.1 convolution_convert_fusion.3
  352.1 4.8 fusion.12
  356.9 5.5 fusion.2
  362.4 2.3 copy-done.38
  367.9 2.1 convert_reduce_fusion.4
  372.2 22.6 %attend_back.2 = (bf16[2,12,4,16,3456]{4,3,2,1,0:T(8,128)(2,1)}, f32[16,192,128]{2,1,0:T(8,128)S(1)}, f32[1,4,3456]{2,1,0:T(4,128)S(1)}) custom-call(bf16[2,12,4,16,3456]{4,3,2,1,0:T(8,128)(2,1)} %add_convert_fusion.mixed_ref, bf16[2,8,4,16,1152]{4,3,2,1,0:T(8,128)(2,1)S(1)} %bitcast.458, f32[16,192,128]{2,1,0:T(8,128)S(1)} %copy-done.1), custom_call_target="tpu_custom_call" | custom-call | tf_op jit(solution)/shard_map/attend_back/pallas_call | solution.py:307
  397.1 4.6 collective-permute-done.45
  401.6 2.7 fusion.66
  408.7 22.5 %attend_back.3 = (bf16[2,12,4,16,3456]{4,3,2,1,0:T(8,128)(2,1)}, f32[16,192,128]{2,1,0:T(8,128)S(1)}, f32[1,4,3456]{2,1,0:T(4,128)S(1)}) custom-call(bf16[2,12,4,16,3456]{4,3,2,1,0:T(8,128)(2,1)} %add_convert_fusion.mixed_ref, bf16[2,8,4,16,1152]{4,3,2,1,0:T(8,128)(2,1)S(1)} %bitcast.459, ...), custom_call_target="tpu_custom_call", output_to_operand_aliasing={{0}: (3, {})} | custom-call | tf_op jit(solution)/shard_map/attend_back/pallas_call | solution.py:307
  438.9 19.5 %fusion.1 = bf16[1152,3456]{1,0:T(8,128)(2,1)} fusion(bf16[2,12,4,16,1152]{4,3,2,1,0:T(8,128)(2,1)} %fusion.16, bf16[2,12,4,16,3456]{4,3,2,1,0:T(8,128)(2,1)} %get-tuple-element.343), kind=kOutput, calls=%fused_computation.11 | convolution fusion | flops 12234571776 | bytes 22118400 | tf_op jit(solution)/shard_map/nd,ne->de/dot_general | solution.py:865
  459.5 2.2 collective-permute-done.50
  462.8 2.3 fusion.63
  469.6 2.5 collective-permute-start.55
  475.2 5.5 bias_sum.1
  482.9 5.1 collective-permute-done.55
  491.5 5.1 collective-permute-start.57
  497.4 11.1 %fusion.27 = f32[1,12,4,16,1152]{4,3,2,1,0:T(8,128)S(1)} fusion(bf16[1152,3456]{1,0:T(8,128)(2,1)} %all-gather.3.cloned.1.call-done, bf16[2,12,4,16,3456]{4,3,2,1,0:T(8,128)(2,1)} %get-tuple-element.343), kind=kOutput, calls=%fused_computation.53 | convolution fusion | flops 6115295232 | bytes 16809984 | tf_op jit(solution)/shard_map/spcge,de->spcgd/dot_general | solution.py:905
  516.8 11.9 %fusion.32 = f32[1,12,4,16,1152]{4,3,2,1,0:T(8,128)S(1)} fusion(bf16[1152,3456]{1,0:T(8,128)(2,1)} %all-gather.3.cloned.1.call-done, bf16[2,12,4,16,3456]{4,3,2,1,0:T(8,128)(2,1)} %get-tuple-element.343), kind=kOutput, calls=%fused_computation.54 | convolution fusion | flops 6115295232 | bytes 16809984 | tf_op jit(solution)/shard_map/spcge,de->spcgd/dot_general | solution.py:905
  528.8 2.8 convert_add_fusion.8
  533.6 3.2 collective-permute-start.60
  537.8 9.2 %fusion.58 = bf16[1,8,4,16,1152]{4,3,2,1,0:T(8,128)(2,1)} fusion(bf16[4608,1152,1,1]{1,0,3,2:T(8,128)(2,1)S(1)} %bitcast.477, bf16[2,8,4,16,4608]{4,3,2,1,0:T(8,128)(2,1)} %copy-done.77, f32[2,8,4,16,1152]{4,3,2,1,0:T(8,128)S(1)} %bitcast.479, f32[1152]{0:T(1024)S(1)} %copy-done.76), kind=kOutput, calls=%fused_computation.64 | convolution fusion | flops 5437587456 | bytes 18878976 | tf_op jit(solution)/shard_map/dot_general | solution.py:29
  548.5 2.2 collective-permute-done.63
  554.9 2.4 collective-permute-done.64
  559.9 2.3 concatenate.30
  565.0 2.8 collective-permute-start.66
  570.6 11.9 %fusion.55 = bf16[1,8,4,16,1152]{4,3,2,1,0:T(8,128)(2,1)S(1)} fusion(bf16[4608,1152,1,1]{1,0,3,2:T(8,128)(2,1)} %bitcast.474, bf16[2,8,4,16,4608]{4,3,2,1,0:T(8,128)(2,1)} %copy-done.77, f32[2,8,4,16,1152]{4,3,2,1,0:T(8,128)} %copy-done.39, f32[1152]{0:T(1024)} %param.40), kind=kOutput, calls=%fused_computation.63 | convolution fusion | flops 5437587456 | bytes 18882560 | tf_op jit(solution)/shard_map/dot_general | solution.py:29
  588.0 1.9 collective-permute-start.72
  598.0 3.4 collective-permute-done.76
  608.8 7.2 %collective-permute-done.78 = bf16[72,3456]{1,0:T(8,128)(2,1)S(1)} collective-permute-done((bf16[72,3456]{1,0:T(8,128)(2,1)}, bf16[72,3456]{1,0:T(8,128)(2,1)S(1)}, u32[]{:S(2)}, u32[]{:S(2)}) %collective-permute-start.78) | collective-permute-done | bytes 497696 | tf_op jit(solution)/shard_map/ppermute | solution.py:341
  (487 shorter events, 139.1 us)
Async XLA Ops:
  7.2 127.5 %all-gather.3.cloned.1.call-start = ((), (), s32[]{:S(2)}) async-start(), calls=%async_computation.3 | async-start | bytes 8460288 | tf_op jit(solution)/shard_map/all_gather | solution.py:718
  8.0 215.4 %all-gather.5.cloned.1.call-start = ((), (), s32[]{:S(2)}) async-start(), calls=%async_computation.4 | async-start | bytes 11280384 | tf_op jit(solution)/shard_map/all_gather | solution.py:772
  24.6 9.2 %collective-permute-start.3 = (bf16[2,2,18,1152]{3,2,0,1:T(8,128)(2,1)S(1)}, bf16[2,2,18,1152]{3,2,0,1:T(8,128)(2,1)S(1)}, u32[]{:S(2)}, u32[]{:S(2)}) collective-permute-start(bf16[2,2,18,1152]{3,2,0,1:T(8,128)(2,1)S(1)} %pad_maximum_fusion.9), channel_id=1, source_target_pairs={{0,4},{2,6},{4,0},{6,2},{8,12},{10,14},{12,8},{14,10},{16,20},{18,... | collective-permute-start | bytes 497672 | tf_op jit(solution)/shard_map/ppermute | solution.py:341
  34.0 9.4 %collective-permute-start.5 = (bf16[72,1152]{1,0:T(8,128)(2,1)S(1)}, bf16[72,1152]{1,0:T(8,128)(2,1)S(1)}, u32[]{:S(2)}, u32[]{:S(2)}) collective-permute-start(bf16[72,1152]{1,0:T(8,128)(2,1)S(1)} %copy-done.14), channel_id=1, source_target_pairs={{0,8},{2,10},{8,16},{10,18},{16,24},{18,26},{24,28},{26,30},{28,20... | collective-permute-start | bytes 497672 | tf_op jit(solution)/shard_map/ppermute | solution.py:420
  35.6 9.6 %collective-permute-start.6 = (bf16[72,1152]{1,0:T(8,128)(2,1)S(1)}, bf16[72,1152]{1,0:T(8,128)(2,1)S(1)}, u32[]{:S(2)}, u32[]{:S(2)}) collective-permute-start(bf16[72,1152]{1,0:T(8,128)(2,1)S(1)} %copy-done.14), channel_id=1, source_target_pairs={{0,4},{2,6},{8,0},{10,2},{16,8},{18,10},{24,16},{26,18},{28,24},{3... | collective-permute-start | bytes 497672 | tf_op jit(solution)/shard_map/ppermute | solution.py:420
  49.5 9.6 %collective-permute-start.9 = (f32[4,72,128]{2,1,0:T(8,128)}, f32[4,72,128]{2,1,0:T(8,128)S(1)}, u32[]{:S(2)}, u32[]{:S(2)}) collective-permute-start(f32[4,72,128]{2,1,0:T(8,128)} %select_bitcast_fusion.13), channel_id=1, source_target_pairs={{0,4},{2,6},{4,0},{6,2},{8,12},{10,14},{12,8},{14,10},{16,20},{18,... | collective-permute-start | bytes 442376 | tf_op jit(solution)/shard_map/ppermute | solution.py:341
  49.7 49.1 %collective-permute-start = (bf16[2,4,4,16,1152]{4,3,2,1,0:T(8,128)(2,1)}, bf16[2,4,4,16,1152]{4,3,2,1,0:T(8,128)(2,1)}, u32[]{:S(2)}, u32[]{:S(2)}) collective-permute-start(bf16[2,4,4,16,1152]{4,3,2,1,0:T(8,128)(2,1)} %constant_dynamic-slice_fusion), channel_id=1, source_target_pairs={{0,1},{1,0},{2,3},{3,2},{4,5},{5,4},{6,7},{7,6},{8,9},{9,8},{10,11... | collective-permute-start | bytes 3538952 | tf_op jit(solution)/shard_map/ppermute | solution.py:68
  51.2 383.6 %reduce-scatter.8.cloned.1.call-start = ((), (), s32[]{:S(2)}) async-start(), calls=%async_computation.5 | async-start | bytes 11280384 | tf_op jit(solution)/shard_map/reduce_scatter | solution.py:815
  69.9 13.9 %collective-permute-start.11 = (f32[1,72,128]{2,1,0:T(8,128)}, f32[1,72,128]{2,1,0:T(8,128)}, u32[]{:S(2)}, u32[]{:S(2)}) collective-permute-start(f32[1,72,128]{2,1,0:T(8,128)} %select_bitcast_fusion.27), channel_id=1, source_target_pairs={{0,16},{2,18},{4,20},{6,22},{8,24},{10,26},{12,28},{14,30},{16,0},... | collective-permute-start | bytes 110600 | tf_op jit(solution)/shard_map/ppermute | solution.py:341
  81.2 9.5 %collective-permute-start.12 = (bf16[72,1152]{1,0:T(8,128)(2,1)S(1)}, bf16[72,1152]{1,0:T(8,128)(2,1)S(1)}, u32[]{:S(2)}, u32[]{:S(2)}) collective-permute-start(bf16[72,1152]{1,0:T(8,128)(2,1)S(1)} %collective-permute-done.5.refs_2_), channel_id=1, source_target_pairs={{0,8},{2,10},{8,16},{10,18},{16,24},{18,26},{24,28},{26,30},{28,20... | collective-permute-start | bytes 497672 | tf_op jit(solution)/shard_map/ppermute | solution.py:420
  83.8 9.7 %collective-permute-start.15 = (bf16[72,1152]{1,0:T(8,128)(2,1)S(1)}, bf16[72,1152]{1,0:T(8,128)(2,1)S(1)}, u32[]{:S(2)}, u32[]{:S(2)}) collective-permute-start(bf16[72,1152]{1,0:T(8,128)(2,1)S(1)} %collective-permute-done.6.refs_4_), channel_id=1, source_target_pairs={{0,2},{2,0},{4,6},{6,4},{8,10},{10,8},{12,14},{14,12},{16,18},{18,... | collective-permute-start | bytes 497672 | tf_op jit(solution)/shard_map/ppermute | solution.py:341
  96.7 36.5 %collective-permute-start.20 = (bf16[72,1152]{1,0:T(8,128)(2,1)S(1)}, bf16[72,1152]{1,0:T(8,128)(2,1)}, u32[]{:S(2)}, u32[]{:S(2)}) collective-permute-start(bf16[72,1152]{1,0:T(8,128)(2,1)S(1)} %collective-permute-done.12.refs_6_), channel_id=1, source_target_pairs={{0,8},{2,10},{8,16},{10,18},{16,24},{18,26},{24,28},{26,30},{28,20... | collective-permute-start | bytes 497672 | tf_op jit(solution)/shard_map/ppermute | solution.py:420
  98.1 35.1 %collective-permute-start.21 = (bf16[72,1152]{1,0:T(8,128)(2,1)S(1)}, bf16[72,1152]{1,0:T(8,128)(2,1)}, u32[]{:S(2)}, u32[]{:S(2)}) collective-permute-start(bf16[72,1152]{1,0:T(8,128)(2,1)S(1)} %collective-permute-done.13.refs_8_), channel_id=1, source_target_pairs={{0,4},{2,6},{8,0},{10,2},{16,8},{18,10},{24,16},{26,18},{28,24},{3... | collective-permute-start | bytes 497672 | tf_op jit(solution)/shard_map/ppermute | solution.py:420
  98.8 34.4 %collective-permute-start.22 = (bf16[72,1152]{1,0:T(8,128)(2,1)S(1)}, bf16[72,1152]{1,0:T(8,128)(2,1)S(1)}, u32[]{:S(2)}, u32[]{:S(2)}) collective-permute-start(bf16[72,1152]{1,0:T(8,128)(2,1)S(1)} %collective-permute-done.12.refs_6_), channel_id=1, source_target_pairs={{0,2},{2,0},{4,6},{6,4},{8,10},{10,8},{12,14},{14,12},{16,18},{18,... | collective-permute-start | bytes 497672 | tf_op jit(solution)/shard_map/ppermute | solution.py:341
  98.8 34.4 %collective-permute-start.23 = (bf16[72,1152]{1,0:T(8,128)(2,1)S(1)}, bf16[72,1152]{1,0:T(8,128)(2,1)S(1)}, u32[]{:S(2)}, u32[]{:S(2)}) collective-permute-start(bf16[72,1152]{1,0:T(8,128)(2,1)S(1)} %collective-permute-done.13.refs_8_), channel_id=1, source_target_pairs={{0,2},{2,0},{4,6},{6,4},{8,10},{10,8},{12,14},{14,12},{16,18},{18,... | collective-permute-start | bytes 497672 | tf_op jit(solution)/shard_map/ppermute | solution.py:341
  102.4 11.3 %collective-permute-start.17 = (bf16[4,8,3456]{2,1,0:T(8,128)(2,1)S(1)}, bf16[4,8,3456]{2,1,0:T(8,128)(2,1)S(1)}, u32[]{:S(2)}, u32[]{:S(2)}) collective-permute-start(bf16[4,8,3456]{2,1,0:T(8,128)(2,1)S(1)} %fusion.74), channel_id=1, source_target_pairs={{0,4},{2,6},{4,0},{6,2},{8,12},{10,14},{12,8},{14,10},{16,20},{18,... | collective-permute-start | bytes 663560 | tf_op jit(solution)/shard_map/ppermute | solution.py:341
  113.8 10.9 %collective-permute-start.18 = (bf16[2,8,3456]{2,1,0:T(8,128)(2,1)S(1)}, bf16[2,8,3456]{2,1,0:T(8,128)(2,1)S(1)}, u32[]{:S(2)}, u32[]{:S(2)}) collective-permute-start(bf16[2,8,3456]{2,1,0:T(8,128)(2,1)S(1)} %fusion.80), channel_id=1, source_target_pairs={{0,8},{2,10},{4,12},{6,14},{8,0},{10,2},{12,4},{14,6},{16,24},{18,... | collective-permute-start | bytes 331784 | tf_op jit(solution)/shard_map/ppermute | solution.py:341
  133.3 21.6 %collective-permute-start.24 = (bf16[72,1152]{1,0:T(8,128)(2,1)}, bf16[72,1152]{1,0:T(8,128)(2,1)}, u32[]{:S(2)}, u32[]{:S(2)}) collective-permute-start(bf16[72,1152]{1,0:T(8,128)(2,1)} %collective-permute-done.20.refs_10_), channel_id=1, source_target_pairs={{0,8},{2,10},{8,16},{10,18},{16,24},{18,26},{24,28},{26,30},{28,20... | collective-permute-start | bytes 497672 | tf_op jit(solution)/shard_map/ppermute | solution.py:420
  133.8 21.1 %collective-permute-start.25 = (bf16[72,1152]{1,0:T(8,128)(2,1)}, bf16[72,1152]{1,0:T(8,128)(2,1)}, u32[]{:S(2)}, u32[]{:S(2)}) collective-permute-start(bf16[72,1152]{1,0:T(8,128)(2,1)} %collective-permute-done.20.refs_10_), channel_id=1, source_target_pairs={{0,2},{2,0},{4,6},{6,4},{8,10},{10,8},{12,14},{14,12},{16,18},{18,... | collective-permute-start | bytes 497672 | tf_op jit(solution)/shard_map/ppermute | solution.py:341
  133.9 21.0 %collective-permute-start.26 = (bf16[72,1152]{1,0:T(8,128)(2,1)}, bf16[72,1152]{1,0:T(8,128)(2,1)}, u32[]{:S(2)}, u32[]{:S(2)}) collective-permute-start(bf16[72,1152]{1,0:T(8,128)(2,1)} %collective-permute-done.21.refs_12_), channel_id=1, source_target_pairs={{0,2},{2,0},{4,6},{6,4},{8,10},{10,8},{12,14},{14,12},{16,18},{18,... | collective-permute-start | bytes 497672 | tf_op jit(solution)/shard_map/ppermute | solution.py:341
  155.0 30.7 %collective-permute-start.27 = (bf16[288,1152]{1,0:T(8,128)(2,1)}, bf16[288,1152]{1,0:T(8,128)(2,1)S(1)}, u32[]{:S(2)}, u32[]{:S(2)}) collective-permute-start(bf16[288,1152]{1,0:T(8,128)(2,1)} %refs_0_.1), channel_id=1, source_target_pairs={{0,8},{2,10},{8,16},{10,18},{16,24},{18,26},{24,28},{26,30},{28,20... | collective-permute-start | bytes 1990664 | tf_op jit(solution)/shard_map/ppermute | solution.py:420
  155.0 42.5 %collective-permute-start.28 = (bf16[288,1152]{1,0:T(8,128)(2,1)}, bf16[288,1152]{1,0:T(8,128)(2,1)S(1)}, u32[]{:S(2)}, u32[]{:S(2)}) collective-permute-start(bf16[288,1152]{1,0:T(8,128)(2,1)} %refs_0_.1), channel_id=1, source_target_pairs={{0,4},{2,6},{8,0},{10,2},{16,8},{18,10},{24,16},{26,18},{28,24},{3... | collective-permute-start | bytes 1990664 | tf_op jit(solution)/shard_map/ppermute | solution.py:420
  157.0 40.5 %collective-permute-start.29 = (bf16[288,1152]{1,0:T(8,128)(2,1)}, bf16[288,1152]{1,0:T(8,128)(2,1)}, u32[]{:S(2)}, u32[]{:S(2)}) collective-permute-start(bf16[288,1152]{1,0:T(8,128)(2,1)} %refs_0_.1), channel_id=1, source_target_pairs={{0,2},{2,0},{4,6},{6,4},{8,10},{10,8},{12,14},{14,12},{16,18},{18,... | collective-permute-start | bytes 1990664 | tf_op jit(solution)/shard_map/ppermute | solution.py:341
  157.0 28.6 %collective-permute-start.30 = (bf16[72,1152]{1,0:T(8,128)(2,1)}, bf16[72,1152]{1,0:T(8,128)(2,1)}, u32[]{:S(2)}, u32[]{:S(2)}) collective-permute-start(bf16[72,1152]{1,0:T(8,128)(2,1)} %collective-permute-done.24.refs_14_), channel_id=1, source_target_pairs={{0,2},{2,0},{4,6},{6,4},{8,10},{10,8},{12,14},{14,12},{16,18},{18,... | collective-permute-start | bytes 497672 | tf_op jit(solution)/shard_map/ppermute | solution.py:341
  200.3 18.6 %collective-permute-start.31 = (bf16[288,1152]{1,0:T(8,128)(2,1)S(1)}, bf16[288,1152]{1,0:T(8,128)(2,1)}, u32[]{:S(2)}, u32[]{:S(2)}) collective-permute-start(bf16[288,1152]{1,0:T(8,128)(2,1)S(1)} %collective-permute-done.27.refs_0_), channel_id=1, source_target_pairs={{0,8},{2,10},{8,16},{10,18},{16,24},{18,26},{24,28},{26,30},{28,20... | collective-permute-start | bytes 1990664 | tf_op jit(solution)/shard_map/ppermute | solution.py:420
  202.0 16.9 %collective-permute-start.32 = (bf16[288,1152]{1,0:T(8,128)(2,1)S(1)}, bf16[288,1152]{1,0:T(8,128)(2,1)}, u32[]{:S(2)}, u32[]{:S(2)}) collective-permute-start(bf16[288,1152]{1,0:T(8,128)(2,1)S(1)} %collective-permute-done.28.refs_2_), channel_id=1, source_target_pairs={{0,4},{2,6},{8,0},{10,2},{16,8},{18,10},{24,16},{26,18},{28,24},{3... | collective-permute-start | bytes 1990664 | tf_op jit(solution)/shard_map/ppermute | solution.py:420
  202.4 16.6 %collective-permute-start.33 = (bf16[288,1152]{1,0:T(8,128)(2,1)S(1)}, bf16[288,1152]{1,0:T(8,128)(2,1)S(1)}, u32[]{:S(2)}, u32[]{:S(2)}) collective-permute-start(bf16[288,1152]{1,0:T(8,128)(2,1)S(1)} %collective-permute-done.27.refs_0_), channel_id=1, source_target_pairs={{0,2},{2,0},{4,6},{6,4},{8,10},{10,8},{12,14},{14,12},{16,18},{18,... | collective-permute-start | bytes 1990664 | tf_op jit(solution)/shard_map/ppermute | solution.py:341
  202.4 17.4 %collective-permute-start.34 = (bf16[288,1152]{1,0:T(8,128)(2,1)S(1)}, bf16[288,1152]{1,0:T(8,128)(2,1)S(1)}, u32[]{:S(2)}, u32[]{:S(2)}) collective-permute-start(bf16[288,1152]{1,0:T(8,128)(2,1)S(1)} %collective-permute-done.28.refs_2_), channel_id=1, source_target_pairs={{0,2},{2,0},{4,6},{6,4},{8,10},{10,8},{12,14},{14,12},{16,18},{18,... | collective-permute-start | bytes 1990664 | tf_op jit(solution)/shard_map/ppermute | solution.py:341
  220.6 29.0 %collective-permute-start.35 = (bf16[288,1152]{1,0:T(8,128)(2,1)}, bf16[288,1152]{1,0:T(8,128)(2,1)}, u32[]{:S(2)}, u32[]{:S(2)}) collective-permute-start(bf16[288,1152]{1,0:T(8,128)(2,1)} %collective-permute-done.31.refs_4_), channel_id=1, source_target_pairs={{0,8},{2,10},{8,16},{10,18},{16,24},{18,26},{24,28},{26,30},{28,20... | collective-permute-start | bytes 1990664 | tf_op jit(solution)/shard_map/ppermute | solution.py:420
  222.3 27.3 %collective-permute-start.36 = (bf16[288,1152]{1,0:T(8,128)(2,1)}, bf16[288,1152]{1,0:T(8,128)(2,1)}, u32[]{:S(2)}, u32[]{:S(2)}) collective-permute-start(bf16[288,1152]{1,0:T(8,128)(2,1)} %collective-permute-done.32.refs_6_), channel_id=1, source_target_pairs={{0,4},{2,6},{8,0},{10,2},{16,8},{18,10},{24,16},{26,18},{28,24},{3... | collective-permute-start | bytes 1990664 | tf_op jit(solution)/shard_map/ppermute | solution.py:420
  222.8 26.8 %collective-permute-start.37 = (bf16[288,1152]{1,0:T(8,128)(2,1)}, bf16[288,1152]{1,0:T(8,128)(2,1)}, u32[]{:S(2)}, u32[]{:S(2)}) collective-permute-start(bf16[288,1152]{1,0:T(8,128)(2,1)} %collective-permute-done.31.refs_4_), channel_id=1, source_target_pairs={{0,2},{2,0},{4,6},{6,4},{8,10},{10,8},{12,14},{14,12},{16,18},{18,... | collective-permute-start | bytes 1990664 | tf_op jit(solution)/shard_map/ppermute | solution.py:341
  222.8 26.8 %collective-permute-start.38 = (bf16[288,1152]{1,0:T(8,128)(2,1)}, bf16[288,1152]{1,0:T(8,128)(2,1)}, u32[]{:S(2)}, u32[]{:S(2)}) collective-permute-start(bf16[288,1152]{1,0:T(8,128)(2,1)} %collective-permute-done.32.refs_6_), channel_id=1, source_target_pairs={{0,2},{2,0},{4,6},{6,4},{8,10},{10,8},{12,14},{14,12},{16,18},{18,... | collective-permute-start | bytes 1990664 | tf_op jit(solution)/shard_map/ppermute | solution.py:341
  249.6 18.4 %collective-permute-start.39 = (bf16[288,1152]{1,0:T(8,128)(2,1)}, bf16[288,1152]{1,0:T(8,128)(2,1)}, u32[]{:S(2)}, u32[]{:S(2)}) collective-permute-start(bf16[288,1152]{1,0:T(8,128)(2,1)} %collective-permute-done.35.refs_8_), channel_id=1, source_target_pairs={{0,8},{2,10},{8,16},{10,18},{16,24},{18,26},{24,28},{26,30},{28,20... | collective-permute-start | bytes 1990664 | tf_op jit(solution)/shard_map/ppermute | solution.py:420
  251.4 16.7 %collective-permute-start.40 = (bf16[288,1152]{1,0:T(8,128)(2,1)}, bf16[288,1152]{1,0:T(8,128)(2,1)}, u32[]{:S(2)}, u32[]{:S(2)}) collective-permute-start(bf16[288,1152]{1,0:T(8,128)(2,1)} %collective-permute-done.35.refs_8_), channel_id=1, source_target_pairs={{0,2},{2,0},{4,6},{6,4},{8,10},{10,8},{12,14},{14,12},{16,18},{18,... | collective-permute-start | bytes 1990664 | tf_op jit(solution)/shard_map/ppermute | solution.py:341
  251.4 16.7 %collective-permute-start.41 = (bf16[288,1152]{1,0:T(8,128)(2,1)}, bf16[288,1152]{1,0:T(8,128)(2,1)}, u32[]{:S(2)}, u32[]{:S(2)}) collective-permute-start(bf16[288,1152]{1,0:T(8,128)(2,1)} %collective-permute-done.36.refs_10_), channel_id=1, source_target_pairs={{0,2},{2,0},{4,6},{6,4},{8,10},{10,8},{12,14},{14,12},{16,18},{18,... | collective-permute-start | bytes 1990664 | tf_op jit(solution)/shard_map/ppermute | solution.py:341
  268.3 295.0 %reduce-scatter.10.cloned.1.call-start = ((), (), s32[]{:S(2)}) async-start(), calls=%async_computation.6 | async-start | bytes 2820096
  341.5 15.4 %collective-permute-start.43 = (bf16[8,72,4608]{2,1,0:T(8,128)(2,1)}, bf16[8,72,4608]{2,1,0:T(8,128)(2,1)}, u32[]{:S(2)}, u32[]{:S(2)}) collective-permute-start(bf16[8,72,4608]{2,1,0:T(8,128)(2,1)} %dynamic-slice_bitcast_fusion), channel_id=1, source_target_pairs={{0,2},{2,0},{4,6},{6,4},{8,10},{10,8},{12,14},{14,12},{16,18},{18,... | collective-permute-start | bytes 15925256 | tf_op jit(solution)/shard_map/ppermute | solution.py:341
  365.8 31.2 %collective-permute-start.44 = (bf16[72,4608]{1,0:T(8,128)(2,1)}, bf16[72,4608]{1,0:T(8,128)(2,1)S(1)}, u32[]{:S(2)}, u32[]{:S(2)}) collective-permute-start(bf16[72,4608]{1,0:T(8,128)(2,1)} %get-tuple-element.303), channel_id=1, source_target_pairs={{0,8},{2,10},{8,16},{10,18},{16,24},{18,26},{24,28},{26,30},{28,20... | collective-permute-start | bytes 1990664 | tf_op jit(solution)/shard_map/ppermute | solution.py:498
  367.5 34.2 %collective-permute-start.45 = (bf16[72,4608]{1,0:T(8,128)(2,1)}, bf16[72,4608]{1,0:T(8,128)(2,1)S(1)}, u32[]{:S(2)}, u32[]{:S(2)}) collective-permute-start(bf16[72,4608]{1,0:T(8,128)(2,1)} %get-tuple-element.304), channel_id=1, source_target_pairs={{0,4},{2,6},{8,0},{10,2},{16,8},{18,10},{24,16},{26,18},{28,24},{3... | collective-permute-start | bytes 1990664 | tf_op jit(solution)/shard_map/ppermute | solution.py:498
  404.4 28.0 %collective-permute-start.46 = (bf16[72,4608]{1,0:T(8,128)(2,1)}, bf16[72,4608]{1,0:T(8,128)(2,1)S(1)}, u32[]{:S(2)}, u32[]{:S(2)}) collective-permute-start(bf16[72,4608]{1,0:T(8,128)(2,1)} %get-tuple-element.313), channel_id=1, source_target_pairs={{0,8},{2,10},{8,16},{10,18},{16,24},{18,26},{24,28},{26,30},{28,20... | collective-permute-start | bytes 1990664 | tf_op jit(solution)/shard_map/ppermute | solution.py:498
  405.2 27.2 %collective-permute-start.47 = (bf16[72,4608]{1,0:T(8,128)(2,1)}, bf16[72,4608]{1,0:T(8,128)(2,1)S(1)}, u32[]{:S(2)}, u32[]{:S(2)}) collective-permute-start(bf16[72,4608]{1,0:T(8,128)(2,1)} %get-tuple-element.314), channel_id=1, source_target_pairs={{0,4},{2,6},{8,0},{10,2},{16,8},{18,10},{24,16},{26,18},{28,24},{3... | collective-permute-start | bytes 1990664 | tf_op jit(solution)/shard_map/ppermute | solution.py:498
  407.0 195.4 %reduce-scatter.12.cloned.1.call-start = ((), (), s32[]{:S(2)}) async-start(), calls=%async_computation.7 | async-start | bytes 8460288
  434.8 23.6 %collective-permute-start.48 = (f32[2,4,3456]{2,1,0:T(4,128)}, f32[2,4,3456]{2,1,0:T(4,128)S(1)}, u32[]{:S(2)}, u32[]{:S(2)}) collective-permute-start(f32[2,4,3456]{2,1,0:T(4,128)} %pad_maximum_fusion.14), channel_id=1, source_target_pairs={{0,1},{1,0},{2,3},{3,2},{4,5},{5,4},{6,7},{7,6},{8,9},{9,8},{10,11... | collective-permute-start | bytes 331784 | tf_op jit(solution)/shard_map/ppermute | solution.py:341
  436.3 23.1 %collective-permute-start.49 = (bf16[72,4608]{1,0:T(8,128)(2,1)S(1)}, bf16[72,4608]{1,0:T(8,128)(2,1)}, u32[]{:S(2)}, u32[]{:S(2)}) collective-permute-start(bf16[72,4608]{1,0:T(8,128)(2,1)S(1)} %get-tuple-element.324), channel_id=1, source_target_pairs={{0,8},{2,10},{8,16},{10,18},{16,24},{18,26},{24,28},{26,30},{28,20... | collective-permute-start | bytes 1990664 | tf_op jit(solution)/shard_map/ppermute | solution.py:498
  437.1 24.5 %collective-permute-start.50 = (bf16[72,4608]{1,0:T(8,128)(2,1)S(1)}, bf16[72,4608]{1,0:T(8,128)(2,1)S(1)}, u32[]{:S(2)}, u32[]{:S(2)}) collective-permute-start(bf16[72,4608]{1,0:T(8,128)(2,1)S(1)} %get-tuple-element.325), channel_id=1, source_target_pairs={{0,4},{2,6},{8,0},{10,2},{16,8},{18,10},{24,16},{26,18},{28,24},{3... | collective-permute-start | bytes 1990664 | tf_op jit(solution)/shard_map/ppermute | solution.py:498
  438.3 23.3 %collective-permute-start.51 = (bf16[288,1152]{1,0:T(8,128)(2,1)}, bf16[288,1152]{1,0:T(8,128)(2,1)S(1)}, u32[]{:S(2)}, u32[]{:S(2)}) collective-permute-start(bf16[288,1152]{1,0:T(8,128)(2,1)} %reduce-scatter.8.cloned.1.call-done), channel_id=1, source_target_pairs={{0,1},{1,0},{2,3},{3,2},{4,5},{5,4},{6,7},{7,6},{8,9},{9,8},{10,11... | collective-permute-start | bytes 1990664 | tf_op jit(solution)/shard_map/ppermute | solution.py:341
  465.1 24.2 %collective-permute-start.52 = (bf16[72,4608]{1,0:T(8,128)(2,1)}, bf16[72,4608]{1,0:T(8,128)(2,1)S(1)}, u32[]{:S(2)}, u32[]{:S(2)}) collective-permute-start(bf16[72,4608]{1,0:T(8,128)(2,1)} %fusion.63), channel_id=1, source_target_pairs={{0,8},{2,10},{8,16},{10,18},{16,24},{18,26},{24,28},{26,30},{28,20... | collective-permute-start | bytes 1990664 | tf_op jit(solution)/shard_map/ppermute | solution.py:498
  469.6 18.5 %collective-permute-start.55 = (bf16[8,3456]{1,0:T(8,128)(2,1)S(1)}, bf16[8,3456]{1,0:T(8,128)(2,1)S(1)}, u32[]{:S(2)}, u32[]{:S(2)}) collective-permute-start(bf16[8,3456]{1,0:T(8,128)(2,1)S(1)} %reshape.507), channel_id=1, source_target_pairs={{0,24},{2,26},{4,28},{6,30},{8,16},{10,18},{12,20},{14,22},{16,8},... | collective-permute-start | bytes 165896 | tf_op jit(solution)/shard_map/ppermute | solution.py:341
  472.1 16.6 %collective-permute-start.54 = (bf16[8,3456]{1,0:T(8,128)(2,1)S(1)}, bf16[8,3456]{1,0:T(8,128)(2,1)S(1)}, u32[]{:S(2)}, u32[]{:S(2)}) collective-permute-start(bf16[8,3456]{1,0:T(8,128)(2,1)S(1)} %reshape.507), channel_id=1, source_target_pairs={{0,16},{2,18},{4,20},{6,22},{8,24},{10,26},{12,28},{14,30},{16,0},... | collective-permute-start | bytes 165896 | tf_op jit(solution)/shard_map/ppermute | solution.py:341
  472.7 16.7 %collective-permute-start.53 = (bf16[8,3456]{1,0:T(8,128)(2,1)S(1)}, bf16[8,3456]{1,0:T(8,128)(2,1)S(1)}, u32[]{:S(2)}, u32[]{:S(2)}) collective-permute-start(bf16[8,3456]{1,0:T(8,128)(2,1)S(1)} %reshape.507), channel_id=1, source_target_pairs={{0,8},{2,10},{4,12},{6,14},{8,0},{10,2},{12,4},{14,6},{16,24},{18,... | collective-permute-start | bytes 165896 | tf_op jit(solution)/shard_map/ppermute | solution.py:341
  491.5 22.6 %collective-permute-start.57 = (bf16[2,2,8,3456]{3,2,1,0:T(8,128)(2,1)}, bf16[2,2,8,3456]{3,2,1,0:T(8,128)(2,1)}, u32[]{:S(2)}, u32[]{:S(2)}) collective-permute-start(bf16[2,2,8,3456]{3,2,1,0:T(8,128)(2,1)} %pad_maximum_fusion.10), channel_id=1, source_target_pairs={{0,4},{2,6},{4,0},{6,2},{8,12},{10,14},{12,8},{14,10},{16,20},{18,... | collective-permute-start | bytes 663560 | tf_op jit(solution)/shard_map/ppermute | solution.py:341
  496.6 17.5 %collective-permute-start.56 = (bf16[72,4608]{1,0:T(8,128)(2,1)S(1)}, bf16[72,4608]{1,0:T(8,128)(2,1)}, u32[]{:S(2)}, u32[]{:S(2)}) collective-permute-start(bf16[72,4608]{1,0:T(8,128)(2,1)S(1)} %fusion.65), channel_id=1, source_target_pairs={{0,1},{1,0},{2,3},{3,2},{4,5},{5,4},{6,7},{7,6},{8,9},{9,8},{10,11... | collective-permute-start | bytes 1990664 | tf_op jit(solution)/shard_map/ppermute | solution.py:341
  515.3 16.4 %collective-permute-start.58 = (bf16[2,2,2,8,3456]{4,3,2,1,0:T(8,128)(2,1)S(1)}, bf16[2,2,2,8,3456]{4,3,2,1,0:T(8,128)(2,1)S(1)}, u32[]{:S(2)}, u32[]{:S(2)}) collective-permute-start(bf16[2,2,2,8,3456]{4,3,2,1,0:T(8,128)(2,1)S(1)} %pad_maximum_fusion.6), channel_id=1, source_target_pairs={{0,2},{2,0},{4,6},{6,4},{8,10},{10,8},{12,14},{14,12},{16,18},{18,... | collective-permute-start | bytes 1327112 | tf_op jit(solution)/shard_map/ppermute | solution.py:341
  515.3 16.3 %collective-permute-start.59 = (bf16[1,4,4,16,1152]{4,3,2,1,0:T(8,128)(2,1)}, bf16[1,4,4,16,1152]{4,3,2,1,0:T(8,128)(2,1)S(1)}, u32[]{:S(2)}, u32[]{:S(2)}) collective-permute-start(bf16[1,4,4,16,1152]{4,3,2,1,0:T(8,128)(2,1)} %slice.362), channel_id=1, source_target_pairs={{0,1},{1,0},{2,3},{3,2},{4,5},{5,4},{6,7},{7,6},{8,9},{9,8},{10,11... | collective-permute-start | bytes 1769480 | tf_op jit(solution)/shard_map/ppermute | solution.py:627
  532.3 16.1 %collective-permute-start.62 = (bf16[72,128]{1,0:T(8,128)(2,1)S(1)}, bf16[72,128]{1,0:T(8,128)(2,1)S(1)}, u32[]{:S(2)}, u32[]{:S(2)}) collective-permute-start(bf16[72,128]{1,0:T(8,128)(2,1)S(1)} %fusion.68), channel_id=1, source_target_pairs={{0,24},{2,26},{4,28},{6,30},{8,16},{10,18},{12,20},{14,22},{16,8},... | collective-permute-start | bytes 55304 | tf_op jit(solution)/shard_map/ppermute | solution.py:341
  533.1 15.4 %collective-permute-start.61 = (bf16[72,128]{1,0:T(8,128)(2,1)S(1)}, bf16[72,128]{1,0:T(8,128)(2,1)S(1)}, u32[]{:S(2)}, u32[]{:S(2)}) collective-permute-start(bf16[72,128]{1,0:T(8,128)(2,1)S(1)} %fusion.68), channel_id=1, source_target_pairs={{0,16},{2,18},{4,20},{6,22},{8,24},{10,26},{12,28},{14,30},{16,0},... | collective-permute-start | bytes 55304 | tf_op jit(solution)/shard_map/ppermute | solution.py:341
  533.6 14.9 %collective-permute-start.60 = (bf16[72,128]{1,0:T(8,128)(2,1)S(1)}, bf16[72,128]{1,0:T(8,128)(2,1)S(1)}, u32[]{:S(2)}, u32[]{:S(2)}) collective-permute-start(bf16[72,128]{1,0:T(8,128)(2,1)S(1)} %fusion.68), channel_id=1, source_target_pairs={{0,8},{2,10},{4,12},{6,14},{8,0},{10,2},{12,4},{14,6},{16,24},{18,... | collective-permute-start | bytes 55304 | tf_op jit(solution)/shard_map/ppermute | solution.py:341
  536.8 13.9 %collective-permute-start.63 = (bf16[1,4,4,16,1152]{4,3,2,1,0:T(8,128)(2,1)S(1)}, bf16[1,4,4,16,1152]{4,3,2,1,0:T(8,128)(2,1)S(1)}, u32[]{:S(2)}, u32[]{:S(2)}) collective-permute-start(bf16[1,4,4,16,1152]{4,3,2,1,0:T(8,128)(2,1)S(1)} %slice.361), channel_id=1, source_target_pairs={{0,1},{1,0},{2,3},{3,2},{4,5},{5,4},{6,7},{7,6},{8,9},{9,8},{10,11... | collective-permute-start | bytes 1769480 | tf_op jit(solution)/shard_map/ppermute | solution.py:627
  563.3 21.2 %collective-permute-start.68 = (bf16[72,128]{1,0:T(8,128)(2,1)S(1)}, bf16[72,128]{1,0:T(8,128)(2,1)}, u32[]{:S(2)}, u32[]{:S(2)}) collective-permute-start(bf16[72,128]{1,0:T(8,128)(2,1)S(1)} %fusion.90), channel_id=1, source_target_pairs={{0,24},{2,26},{4,28},{6,30},{8,16},{10,18},{12,20},{14,22},{16,8},... | collective-permute-start | bytes 55304 | tf_op jit(solution)/shard_map/ppermute | solution.py:341
  564.2 20.4 %collective-permute-start.67 = (bf16[72,128]{1,0:T(8,128)(2,1)S(1)}, bf16[72,128]{1,0:T(8,128)(2,1)}, u32[]{:S(2)}, u32[]{:S(2)}) collective-permute-start(bf16[72,128]{1,0:T(8,128)(2,1)S(1)} %fusion.90), channel_id=1, source_target_pairs={{0,16},{2,18},{4,20},{6,22},{8,24},{10,26},{12,28},{14,30},{16,0},... | collective-permute-start | bytes 55304 | tf_op jit(solution)/shard_map/ppermute | solution.py:341
  565.0 19.6 %collective-permute-start.66 = (bf16[72,128]{1,0:T(8,128)(2,1)S(1)}, bf16[72,128]{1,0:T(8,128)(2,1)}, u32[]{:S(2)}, u32[]{:S(2)}) collective-permute-start(bf16[72,128]{1,0:T(8,128)(2,1)S(1)} %fusion.90), channel_id=1, source_target_pairs={{0,8},{2,10},{4,12},{6,14},{8,0},{10,2},{12,4},{14,6},{16,24},{18,... | collective-permute-start | bytes 55304 | tf_op jit(solution)/shard_map/ppermute | solution.py:341
  567.8 16.8 %collective-permute-start.69 = (f32[12,1152]{1,0:T(8,128)S(1)}, f32[12,1152]{1,0:T(8,128)}, u32[]{:S(2)}, u32[]{:S(2)}) collective-permute-start(f32[12,1152]{1,0:T(8,128)S(1)} %concatenate.30), channel_id=1, source_target_pairs={{0,2},{2,0},{4,6},{6,4},{8,10},{10,8},{12,14},{14,12},{16,18},{18,... | collective-permute-start | bytes 165896 | tf_op jit(solution)/shard_map/ppermute | solution.py:341
  567.8 16.8 %collective-permute-start.70 = (bf16[72,1152]{1,0:T(8,128)(2,1)}, bf16[72,1152]{1,0:T(8,128)(2,1)}, u32[]{:S(2)}, u32[]{:S(2)}) collective-permute-start(bf16[72,1152]{1,0:T(8,128)(2,1)} %reduce-scatter.10.cloned.1.call-done), channel_id=1, source_target_pairs={{0,1},{1,0},{2,3},{3,2},{4,5},{5,4},{6,7},{7,6},{8,9},{9,8},{10,11... | collective-permute-start | bytes 497672 | tf_op jit(solution)/shard_map/ppermute | solution.py:341
  602.4 13.6 %collective-permute-start.78 = (bf16[72,3456]{1,0:T(8,128)(2,1)}, bf16[72,3456]{1,0:T(8,128)(2,1)S(1)}, u32[]{:S(2)}, u32[]{:S(2)}) collective-permute-start(bf16[72,3456]{1,0:T(8,128)(2,1)} %reduce-scatter.12.cloned.1.call-done), channel_id=1, source_target_pairs={{0,1},{1,0},{2,3},{3,2},{4,5},{5,4},{6,7},{7,6},{8,9},{9,8},{10,11... | collective-permute-start | bytes 1493000 | tf_op jit(solution)/shard_map/ppermute | solution.py:341
  (108 other events, 1240.5 us)
Sparse Core Ops, SparseCore 0:
  10.2 83.8 all-gather.2
  96.4 101.1 all-gather.4
  268.4 132.3 reduce-scatter.7
  407.1 74.9 reduce-scatter.9
  486.6 105.8 reduce-scatter.11
